TPU v7x, 128 devices: a whole 4x4x4 slice. The times are simulated.
128 devices in a mesh: row: 16 (over y, z_hi, core), col: 8 (over x, z_lo).
Axes of the slice: x: 4, y: 4, z: 4 (z_hi: 2, z_lo: 2; z = z_hi * 2 + z_lo), core: 2. Of those that a mesh axis runs over, the one named last changes fastest.
Arguments:
- orbitals: bfloat16 [24576, 2, 2048], P(('row', 'col')), may hold values from -6 to 6
- applied_orbitals: bfloat16 [24576, 2, 2048], P(('row', 'col')), may hold values from -6 to 6
- ritz_matrix: bfloat16 [2, 2048, 2048], P(None, 'row', 'col'), may hold values from -0.09375 to 0.09375
Outputs:
- rotated_orbitals: bfloat16 [24576, 2, 2048], P(('row', 'col'))
- rotated_applied: bfloat16 [24576, 2, 2048], P(('row', 'col'))
All inputs are finite; a program needn't handle non-finite values.
Results may differ from a plain program's by a relative error of at most 0.001.
Values may be sent and summed in bfloat16 or wider, within the bound.
A program may use at most 128 MiB of HBM per device.

v0:
```python
import jax
import jax.numpy as jnp
from jax import lax
from jax.sharding import PartitionSpec as P


def shards(orbitals, applied_orbitals, ritz_matrix):
    row_count = orbitals.shape[0]
    band_count = orbitals.shape[2]
    stacked = jnp.concatenate(
        [
            orbitals.reshape(row_count, 2 * band_count),
            applied_orbitals.reshape(row_count, 2 * band_count),
        ],
        0,
    )
    strip = lax.all_gather(ritz_matrix, "col", axis=2, tiled=True)
    shard_piece = lax.all_gather(strip, "row", axis=1, tiled=True)
    height = shard_piece.shape[1]
    real_cols = lax.slice_in_dim(stacked, 0, height, axis=1)
    imag_cols = lax.dynamic_slice_in_dim(stacked, band_count, height, 1)
    upper_half = jnp.concatenate([shard_piece[0], shard_piece[1]], 1)
    lower_half = jnp.concatenate([-shard_piece[1], shard_piece[0]], 1)
    running = jnp.dot(real_cols, upper_half, preferred_element_type=jnp.float32)
    running = running + jnp.dot(imag_cols, lower_half, preferred_element_type=jnp.float32)
    result = running.reshape(2 * row_count, 2, band_count)
    result = result.astype(jnp.bfloat16)
    return (result[:row_count], result[row_count:])


def solution(mesh):
    in_specs = (P(("row", "col"), None, None), P(("row", "col"), None, None), P(None, "row", "col"))
    out_specs = (P(("row", "col"), None, None), P(("row", "col"), None, None))
    return jax.shard_map(shards, mesh=mesh, in_specs=in_specs, out_specs=out_specs, check_vma=False)
```

profile of v0, /device:TPU:0, one launch (start us, length us, event | category | flops | bytes accessed | tf_op | source)
XLA Modules:
  0.0 228.7 jit_solution(4716080918865581641)
XLA Ops:
  7.2 0.0 all-gather.3.cloned.1.call-start
  7.2 0.7 all-gather.3.cloned.1.call-update
  7.9 0.0 all-gather.5.cloned.1.call-start
  7.9 44.7 %all-gather.3.cloned.1.call-done = bf16[2,128,2048]{2,1,0:T(8,128)(2,1)} async-done(((bf16[2,128,256]{2,1,0:T(8,128)(2,1)}), bf16[2,128,2048]{2,1,0:T(8,128)(2,1)}) %all-gather.3.cloned.1.call-update) | async-done | bytes 1048592 | tf_op jit(solution)/shard_map/all_gather | solution.py:17
  52.7 0.0 all-gather.5.cloned.1.call-update
  52.7 2.1 copy.5
  54.8 2.1 copy.6
  56.8 0.1 constant_dynamic-update-slice_fusion.1
  57.0 0.1 constant_dynamic-update-slice_fusion
  57.1 112.1 %all-gather.5.cloned.1.call-done = bf16[2,2048,2048]{2,1,0:T(8,128)(2,1)} async-done(((bf16[2,128,2048]{2,1,0:T(8,128)(2,1)}), bf16[2,2048,2048]{2,1,0:T(8,128)(2,1)}) %all-gather.5.cloned.1.call-update) | async-done | bytes 16777232 | tf_op jit(solution)/shard_map/all_gather | solution.py:18
  169.2 11.8 %slice_bitcast_fusion.1 = (bf16[2048,2048]{1,0:T(8,128)(2,1)}, bf16[2048,2048]{1,0:T(8,128)(2,1)}) fusion(bf16[2,2048,2048]{2,1,0:T(8,128)(2,1)} %all-gather.5.cloned.1.call-done), kind=kLoop, calls=%fused_computation.9 | loop fusion | bytes 33554432 | tf_op jit(solution)/shard_map/squeeze | solution.py:22
  181.0 12.6 %fusion = f32[384,4096]{1,0:T(8,128)} fusion(bf16[2048,2048]{1,0:T(8,128)(2,1)} %get-tuple-element.3, bf16[2048,2048]{1,0:T(8,128)(2,1)} %get-tuple-element.2, bf16[384,4096]{1,0:T(8,128)(2,1)S(1)} %constant_dynamic-update-slice_fusion), kind=kOutput, calls=%fused_computation | convolution fusion | flops 6476005376 | bytes 24641536 | tf_op jit(solution)/shard_map/dot_general | solution.py:24
  193.6 7.1 %fusion.14 = bf16[2048,2048]{1,0:T(8,128)(2,1)} fusion(bf16[2,2048,2048]{2,1,0:T(8,128)(2,1)} %all-gather.5.cloned.1.call-done), kind=kLoop, calls=%fused_computation.17 | loop fusion | flops 4194304 | bytes 16777216 | tf_op jit(solution)/shard_map/neg | solution.py:23
  200.8 14.3 %add_convert_fusion = bf16[384,4096]{1,0:T(8,128)(2,1)} fusion(f32[384,4096]{1,0:T(8,128)} %fusion, bf16[2048,2048]{1,0:T(8,128)(2,1)} %get-tuple-element.2, bf16[2048,2048]{1,0:T(8,128)(2,1)} %fusion.14, bf16[384,4096]{1,0:T(8,128)(2,1)S(1)} %constant_dynamic-update-slice_fusion), kind=kOutput, calls=%fused_computation.10 | convolution fusion | flops 6479151104 | bytes 27787264 | tf_op jit(solution)/shard_map/dot_general | solution.py:25
  215.1 2.1 fusion.15
  217.2 2.4 %slice.27 = bf16[192,2,2048]{2,1,0:T(2,128)(2,1)} reshape(bf16[192,4096]{1,0:T(8,128)(2,1)S(1)} %get-tuple-element.5) | data formatting | bytes 3145728 | tf_op jit(solution)/shard_map/slice | solution.py:28
  219.5 2.4 %slice.29 = bf16[192,2,2048]{2,1,0:T(2,128)(2,1)} reshape(bf16[192,4096]{1,0:T(8,128)(2,1)S(1)} %get-tuple-element.4) | data formatting | bytes 3145728 | tf_op jit(solution)/shard_map/slice | solution.py:28
Async XLA Ops:
  7.2 45.5 %all-gather.3.cloned.1.call-start = ((), (), s32[]{:S(2)}) async-start(), calls=%async_computation | async-start | bytes 1179648 | tf_op jit(solution)/shard_map/all_gather | solution.py:17
  7.9 161.3 %all-gather.5.cloned.1.call-start = ((), (), s32[]{:S(2)}) async-start(), calls=%async_computation.1 | async-start | bytes 17825792 | tf_op jit(solution)/shard_map/all_gather | solution.py:18
Sparse Core Ops, SparseCore 0:
  9.6 43.0 all-gather.2
  55.1 114.0 all-gather.4
where the time goes:
time: 230 us; the launch traced here: 229 us
  waiting for transfers between devices  158 us (69%)
  matrix products  26.9 us (12%)
  local copies, waits for them, and re-layouts  23 us (10%)
  between operations  14.1 us (6%)
  other arithmetic  7.14 us (3%)
    all_gather x1, waiting for transfers between devices, shards(): shard_piece = lax.all_gather(strip, 'row', axis=1, tiled=True)  112 us
    all_gather x1, waiting for transfers between devices, shards(): strip = lax.all_gather(ritz_matrix, 'col', axis=2, tiled=True)  44.7 us
    dot_general x1, matrix products, shards(): jnp.dot(imag_cols, lower_half, preferred_element_type=jnp.float32)  14.3 us
    dot_general x1, matrix products, shards(): running = jnp.dot(real_cols, upper_half, preferred_element_type=jnp.float32)  12.6 us
    squeeze x1, local copies, waits for them, and re-layouts, shards(): upper_half = jnp.concatenate([shard_piece[0], shard_piece[1]], 1)  11.8 us
    neg x1, other arithmetic, shards(): lower_half = jnp.concatenate([-shard_piece[1], shard_piece[0]], 1)  7.14 us
    slice x3, local copies, waits for them, and re-layouts, shards(): return (result[:row_count], result[row_count:])  6.8 us
  transfers between devices with their start and end apart: 2, of which 2 were waited for; matrix products, arithmetic and copies ran while one was open for 2% of the time, Pallas kernels for 0%

commit v1 on v0

v1 whole, which is shorter than its diff:
```python
import jax
import jax.numpy as jnp
from jax import lax
from jax.sharding import Mesh
from jax.sharding import PartitionSpec as P


def shards(orbitals, applied_orbitals, ritz_matrix):
    me = lax.axis_index("core")
    other = 1 - me
    rows = orbitals.shape[0]
    band_count = orbitals.shape[2]
    cols = ritz_matrix.shape[2]
    half = cols // 2
    col_blocks = band_count // cols

    stacked = jnp.stack([orbitals, applied_orbitals])
    both = lax.all_gather(stacked, "core")
    chip_block = lax.all_gather(ritz_matrix, "core")
    mine = lax.dynamic_slice_in_dim(chip_block, me * half, half, axis=3)
    gathered = lax.all_gather(mine, ("col", "rc"))
    gathered = gathered.reshape(col_blocks, -1, 2, 2, ritz_matrix.shape[1], half)

    lhs = both.reshape(2, 2, rows, 2, -1, 2, ritz_matrix.shape[1])
    prod = jnp.einsum(
        "xanqrok,cropkj->xanqpcj", lhs, gathered, preferred_element_type=jnp.float32
    )
    real = prod[:, :, :, 0, 0] - prod[:, :, :, 1, 1]
    imag = prod[:, :, :, 0, 1] + prod[:, :, :, 1, 0]
    result = jnp.stack([real, imag], 3).astype(jnp.bfloat16)

    own = lax.dynamic_index_in_dim(result, me, 0, keepdims=False)
    send = lax.dynamic_index_in_dim(result, other, 0, keepdims=False)
    recv = lax.ppermute(send, "core", [(0, 1), (1, 0)])
    first = jnp.where(me == 0, own, recv)
    second = jnp.where(me == 0, recv, own)
    out = jnp.stack([first, second], -2).reshape(2, rows, 2, band_count)
    return out[0], out[1]


def solution(mesh):
    devices = mesh.devices
    split = Mesh(
        devices.reshape(devices.shape[0] // 2, 2, devices.shape[1]), ("rc", "core", "col")
    )
    flat = ("rc", "core", "col")
    in_specs = (P(flat, None, None), P(flat, None, None), P(None, ("rc", "core"), "col"))
    out_specs = (P(flat, None, None), P(flat, None, None))
    return jax.shard_map(shards, mesh=split, in_specs=in_specs, out_specs=out_specs, check_vma=False)
```

time: 230 us -> 432 us (1.88)
  waiting for transfers between devices: 158 us -> 364 us
  matrix products: 26.9 us -> 19 us
    all_gather x2, waiting for transfers between devices: 157 us -> 360 us  [the longest x1 341 us: shards(): gathered = lax.all_gather(mine, ('col', 'rc'))]
    squeeze x1 -> x0, local copies, waits for them, and re-layouts: 11.8 us -> none  [shards(): upper_half = jnp.concatenate([shard_piece[0], shard_piece[1]], 1)]
    reshape x0 -> x1, local copies, waits for them, and re-layouts: none -> 11 us  [shards(): lhs = both.reshape(2, 2, rows, 2, -1, 2, ritz_matrix.shape[1])]
    dot_general x2 -> x1, matrix products: 26.9 us -> 19 us  [shards(): jnp.einsum('xanqrok,cropkj->xanqpcj', lhs, gathered, preferred_element_ty...]
    neg x1 -> x0, other arithmetic: 7.14 us -> none  [shards(): lower_half = jnp.concatenate([-shard_piece[1], shard_piece[0]], 1)]
    slice x3 -> x0, local copies, waits for them, and re-layouts: 6.8 us -> none  [shards(): return (result[:row_count], result[row_count:])]
    unnamed x3 -> x6, local copies, waits for them, and re-layouts: 4.25 us -> 9.39 us
    another operation x0 -> x4, other arithmetic: none -> 4.82 us  [the longest x2 2.64 us: shards(): out = jnp.stack([first, second], -2).reshape(2, rows, 2, band_count)]
  transfers between devices with their start and end apart: 2 -> 3, of which waited for: 2 -> 3; matrix products, arithmetic and copies ran while one was open for 2% -> 3% of each run, Pallas kernels for 0% -> 0%
where the time goes in v1:
time: 432 us; the launch traced here: 430 us
  waiting for transfers between devices  364 us (84%)
  local copies, waits for them, and re-layouts  25.3 us (6%)
  matrix products  19 us (4%)
  between operations  14.1 us (3%)
  other arithmetic  5.82 us (1%)
    all_gather x1, waiting for transfers between devices, shards(): gathered = lax.all_gather(mine, ('col', 'rc'))  341 us
    dot_general x1, matrix products, shards(): jnp.einsum('xanqrok,cropkj->xanqpcj', lhs, gathered, preferred_element_ty...  19 us
    all_gather x1, waiting for transfers between devices, shards(): both = lax.all_gather(stacked, 'core')  18.5 us
    reshape x1, local copies, waits for them, and re-layouts, shards(): lhs = both.reshape(2, 2, rows, 2, -1, 2, ritz_matrix.shape[1])  11 us
    unnamed x6, local copies, waits for them, and re-layouts  9.39 us
  transfers between devices with their start and end apart: 3, of which 3 were waited for; matrix products, arithmetic and copies ran while one was open for 3% of the time, Pallas kernels for 0%

profile of v1, /device:TPU:0, one launch (start us, length us, event | category | flops | bytes accessed | tf_op | source)
XLA Modules:
  0.0 430.1 jit_solution(7982610244307542527)
XLA Ops:
  7.2 0.0 all-gather.8.cloned.1.call-start
  7.2 3.2 copy_bitcast_fusion.1
  10.5 1.9 pad_maximum_fusion
  12.4 0.0 copy-start
  12.4 0.0 all-gather.8.cloned.1.call-update
  12.4 0.0 all-gather.6.cloned.1.call-start
  12.4 0.8 copy-done
  13.3 2.0 all-gather
  15.2 0.7 constant_dynamic-slice_fusion
  15.9 0.0 all-gather.6.cloned.1.call-update
  15.9 18.5 %all-gather.8.cloned.1.call-done = bf16[4,192,2,2048]{3,1,2,0:T(8,128)(2,1)} async-done(((bf16[2,192,2,2048]{3,1,2,0:T(8,128)(2,1)}), bf16[4,192,2,2048]{3,1,2,0:T(8,128)(2,1)}) %all-gather.8.cloned.1.call-update) | async-done | bytes 6291472 | tf_op jit(solution)/shard_map/all_gather | solution.py:18
  34.4 11.0 %reshape.54 = bf16[2,2,192,2,8,2,128]{6,5,4,2,3,1,0:T(2,128)(2,1)} reshape(bf16[4,192,2,2048]{3,1,2,0:T(8,128)(2,1)} %all-gather.8.cloned.1.call-done) | data formatting | bytes 12582912 | tf_op jit(solution)/shard_map/reshape | solution.py:24
  45.4 341.5 %all-gather.6.cloned.1.call-done = bf16[128,2,128,128]{3,2,1,0:T(8,128)(2,1)} async-done(((bf16[2,2,128,128]{3,2,1,0:T(8,128)(2,1)}), bf16[128,2,128,128]{3,2,1,0:T(8,128)(2,1)}) %all-gather.6.cloned.1.call-update) | async-done | bytes 8388624 | tf_op jit(solution)/shard_map/all_gather | solution.py:21
  386.9 19.0 %fusion.3 = f32[2,2,192,2,2,8,128]{6,2,3,1,0,4,5:T(8,128)S(1)} fusion(bf16[2,2,192,2,8,2,128,1,1]{6,5,4,2,3,1,0,8,7:T(2,128)(2,1)} %bitcast.51, bf16[8,8,2,2,128,128,1,1,1]{5,4,3,2,1,0,8,7,6:T(8,128)(2,1)} %bitcast.54), kind=kOutput, calls=%fused_computation.3 | convolution fusion | flops 12884901888 | bytes 27262976 | tf_op jit(solution)/shard_map/xanqrok,cropkj->xanqpcj/dot_general | solution.py:25
  405.9 0.5 fusion.12
  406.4 0.5 fusion.13
  406.9 0.3 fusion.15
  407.2 1.0 copy.62
  408.2 0.3 collective-permute-start
  408.5 3.5 collective-permute-done
  412.0 2.4 fusion.17
  414.4 0.3 pad_maximum_fusion.1
  414.7 2.4 copy.43
  417.1 1.9 reshape.63
  419.0 2.4 copy.44
  421.4 1.9 reshape.64
Async XLA Ops:
  7.2 27.3 %all-gather.8.cloned.1.call-start = ((), (), s32[]{:S(2)}) async-start(), calls=%async_computation.1 | async-start | bytes 9437184 | tf_op jit(solution)/shard_map/all_gather | solution.py:18
  12.4 0.9 copy-start
  12.4 374.5 %all-gather.6.cloned.1.call-start = ((), (), s32[]{:S(2)}) async-start(), calls=%async_computation | async-start | bytes 8519680 | tf_op jit(solution)/shard_map/all_gather | solution.py:21
  408.2 3.8 collective-permute-start
Sparse Core Ops, SparseCore 0:
  12.5 21.8 all-gather.7
  36.7 350.1 all-gather.5

commit v2 on v1

--- a/solution.py
+++ b/solution.py
@@ -12,18 +12,17 @@
     band_count = orbitals.shape[2]
     cols = ritz_matrix.shape[2]
     half = cols // 2
-    col_blocks = band_count // cols
 
     stacked = jnp.stack([orbitals, applied_orbitals])
-    both = lax.all_gather(stacked, "core")
+    partner = lax.ppermute(stacked, "core", [(0, 1), (1, 0)])
+    both = jnp.where(me == 0, jnp.stack([stacked, partner]), jnp.stack([partner, stacked]))
     chip_block = lax.all_gather(ritz_matrix, "core")
     mine = lax.dynamic_slice_in_dim(chip_block, me * half, half, axis=3)
-    gathered = lax.all_gather(mine, ("col", "rc"))
-    gathered = gathered.reshape(col_blocks, -1, 2, 2, ritz_matrix.shape[1], half)
+    gathered = lax.all_gather(lax.all_gather(mine, "col"), "rc")
 
     lhs = both.reshape(2, 2, rows, 2, -1, 2, ritz_matrix.shape[1])
     prod = jnp.einsum(
-        "xanqrok,cropkj->xanqpcj", lhs, gathered, preferred_element_type=jnp.float32
+        "xanqrok,rcopkj->xanqpcj", lhs, gathered, preferred_element_type=jnp.float32
     )
     real = prod[:, :, :, 0, 0] - prod[:, :, :, 1, 1]
     imag = prod[:, :, :, 0, 1] + prod[:, :, :, 1, 0]

time: 432 us -> 206 us (0.48)
  waiting for transfers between devices: 364 us -> 133 us
  other arithmetic: 5.82 us -> 10.9 us
    all_gather x2, waiting for transfers between devices: 360 us -> 130 us  [shards(): gathered = lax.all_gather(lax.all_gather(mine, 'col'), 'rc')]
    reshape x1 -> x0, local copies, waits for them, and re-layouts: 11 us -> none  [shards(): lhs = both.reshape(2, 2, rows, 2, -1, 2, ritz_matrix.shape[1])]
    another operation x0 -> x2, local copies, waits for them, and re-layouts: none -> 7.51 us  [shards(): jnp.stack([stacked, partner])]
    another operation x1, other arithmetic: 1.9 us -> 8.43 us  [shards(): stacked = jnp.stack([orbitals, applied_orbitals])]
    unnamed x6 -> x9, local copies, waits for them, and re-layouts: 9.39 us -> 10.9 us
  transfers between devices with their start and end apart: 3 -> 4, of which waited for: 3 -> 3; matrix products, arithmetic and copies ran while one was open for 3% -> 10% of each run, Pallas kernels for 0% -> 0%
where the time goes in v2:
time: 206 us; the launch traced here: 205 us
  waiting for transfers between devices  133 us (65%)
  local copies, waits for them, and re-layouts  24.7 us (12%)
  matrix products  19.2 us (9%)
  between operations  14.2 us (7%)
  other arithmetic  10.9 us (5%)
  blocking collectives  2.21 us (1%)
    all_gather x2, waiting for transfers between devices, shards(): gathered = lax.all_gather(lax.all_gather(mine, 'col'), 'rc')  130 us
    dot_general x1, matrix products, shards(): jnp.einsum('xanqrok,rcopkj->xanqpcj', lhs, gathered, preferred_element_ty...  19.2 us
    unnamed x9, local copies, waits for them, and re-layouts  10.9 us
    another operation x1, other arithmetic, shards(): stacked = jnp.stack([orbitals, applied_orbitals])  8.43 us
    another operation x2, local copies, waits for them, and re-layouts, shards(): jnp.stack([stacked, partner])  7.51 us
    another operation x3, local copies, waits for them, and re-layouts, shards(): stacked = jnp.stack([orbitals, applied_orbitals])  4.57 us
  transfers between devices with their start and end apart: 4, of which 3 were waited for; matrix products, arithmetic and copies ran while one was open for 10% of the time, Pallas kernels for 0%

profile of v2, /device:TPU:0, one launch (start us, length us, event | category | flops | bytes accessed | tf_op | source)
XLA Modules:
  0.0 204.9 jit_solution(18298638649193536291)
XLA Ops:
  7.2 0.0 all-gather.6.cloned.1.call-start
  7.2 2.2 %all-gather = bf16[4,128,256]{2,1,0:T(8,128)(2,1)S(1)} all-gather(bf16[2,128,256]{2,1,0:T(8,128)(2,1)} %param.5), channel_id=2, replica_groups=mesh['rc'=8,'core'=2,'col'=8] {'core'}, dimensions={0}, use_global_device_ids=true | all-gather | bytes 393216 | tf_op jit(solution)/shard_map/all_gather | solution.py:19
  9.4 0.7 constant_dynamic-slice_fusion
  10.1 0.0 all-gather.6.cloned.1.call-update
  10.1 0.0 all-gather.8.cloned.1.call-start
  10.2 41.5 %all-gather.6.cloned.1.call-done = bf16[16,2,128,128]{3,2,1,0:T(8,128)(2,1)} async-done(((bf16[2,2,128,128]{3,2,1,0:T(8,128)(2,1)}), bf16[16,2,128,128]{3,2,1,0:T(8,128)(2,1)}) %all-gather.6.cloned.1.call-update) | async-done | bytes 1048592 | tf_op jit(solution)/shard_map/all_gather | solution.py:21
  51.7 0.0 all-gather.8.cloned.1.call-update
  51.7 0.0 copy-start
  51.7 8.4 %pad_maximum_fusion = bf16[2,192,2,2048]{3,2,1,0:T(2,128)(2,1)} fusion(bf16[1,192,2,2048]{3,2,1,0:T(2,128)(2,1)} %bitcast.53, bf16[1,192,2,2048]{3,2,1,0:T(2,128)(2,1)} %bitcast.52), kind=kLoop, calls=%fused_computation.21 | loop fusion | flops 1572864 | bytes 6291456 | tf_op jit(solution)/shard_map/stack | solution.py:16
  60.2 0.0 collective-permute-start
  60.2 0.0 copy-done
  60.2 1.0 stack.42
  61.2 2.8 %stack.43 = bf16[1,1,192,2,8,2,128]{6,5,4,3,2,1,0:T(2,128)(2,1)S(1)} reshape(bf16[192,2,2048]{2,1,0:T(2,128)(2,1)} %param.4) | data formatting | bytes 3145728 | tf_op jit(solution)/shard_map/stack | solution.py:16
  64.1 0.6 copy_dynamic-update-slice_fusion.1
  64.7 0.7 copy_dynamic-update-slice_fusion
  65.4 0.0 copy-start.1
  65.4 1.7 copy-done.1
  67.1 0.0 collective-permute-done
  67.1 4.6 %stack.48 = bf16[1,2,192,2,8,2,128]{6,5,4,3,2,1,0:T(2,128)(2,1)S(1)} reshape(bf16[2,192,2,2048]{3,2,1,0:T(2,128)(2,1)} %collective-permute-done) | data formatting | bytes 6291456 | tf_op jit(solution)/shard_map/stack | solution.py:18
  71.7 2.9 %copy.34 = bf16[1,2,192,2,8,2,128]{6,2,4,5,3,1,0:T(8,128)(2,1)} copy(bf16[1,2,192,2,8,2,128]{6,5,4,3,2,1,0:T(2,128)(2,1)S(1)} %stack.48) | data formatting | bytes 6291456 | tf_op jit(solution)/shard_map/stack | solution.py:18
  74.6 88.4 %all-gather.8.cloned.1.call-done = bf16[64,2,2,128,128]{4,3,2,1,0:T(8,128)(2,1)} async-done(((bf16[8,2,2,128,128]{4,3,2,1,0:T(8,128)(2,1)}), bf16[64,2,2,128,128]{4,3,2,1,0:T(8,128)(2,1)}) %all-gather.8.cloned.1.call-update) | async-done | bytes 8388624 | tf_op jit(solution)/shard_map/all_gather | solution.py:21
  163.0 19.2 %fusion.10 = f32[2,2,192,2,2,8,128]{6,2,3,1,0,4,5:T(8,128)S(1)} fusion(bf16[1,2,192,2,8,2,128]{6,2,4,5,3,1,0:T(8,128)(2,1)} %copy.34, bf16[1,2,192,2,8,2,128]{6,2,4,5,3,1,0:T(8,128)(2,1)} %copy-done.1, pred[]{:T(512)S(6)} %eq.2, bf16[8,8,2,2,128,128,1,1,1]{5,4,3,2,1,0,8,7,6:T(8,128)(2,1)} %bitcast.57), kind=kOutput, calls=%fused_computation.10 | convolution fusion | flops 12913213440 | bytes 27262976 | tf_op jit(solution)/shard_map/xanqrok,rcopkj->xanqpcj/dot_general | solution.py:24
  182.2 0.5 fusion.19
  182.7 0.5 fusion.20
  183.2 0.3 fusion.22
  183.5 1.0 copy.65
  184.5 0.3 collective-permute-start.1
  184.8 3.4 %collective-permute-done.1 = bf16[2,192,2,8,128]{4,3,2,1,0:T(8,128)(2,1)S(1)} collective-permute-done((bf16[2,192,2,8,128]{4,3,2,1,0:T(8,128)(2,1)S(1)}, bf16[2,192,2,8,128]{4,3,2,1,0:T(8,128)(2,1)S(1)}, u32[]{:S(2)}, u32[]{:S(2)}) %collective-permute-start.1) | collective-permute-done | bytes 1572896 | tf_op jit(solution)/shard_map/ppermute | solution.py:33
  188.2 1.0 fusion.24
  189.2 0.3 pad_maximum_fusion.1
  189.4 2.4 %copy.50 = bf16[1,192,2,8,2,128]{5,4,3,2,1,0:T(2,128)(2,1)S(1)} copy(bf16[1,192,2,8,2,128]{5,3,2,1,0,4:T(8,128)(2,1)S(1)} %get-tuple-element.7) | data formatting | bytes 3145728
  191.9 1.9 reshape.66
  193.7 2.4 %copy.51 = bf16[1,192,2,8,2,128]{5,4,3,2,1,0:T(2,128)(2,1)S(1)} copy(bf16[1,192,2,8,2,128]{5,3,2,1,0,4:T(8,128)(2,1)S(1)} %get-tuple-element.6) | data formatting | bytes 3145728
  196.2 1.9 reshape.67
Async XLA Ops:
  7.2 44.5 %all-gather.6.cloned.1.call-start = ((), (), s32[]{:S(2)}) async-start(), calls=%async_computation | async-start | bytes 1179648 | tf_op jit(solution)/shard_map/all_gather | solution.py:21
  10.1 152.9 %all-gather.8.cloned.1.call-start = ((), (), s32[]{:S(2)}) async-start(), calls=%async_computation.1 | async-start | bytes 9437184 | tf_op jit(solution)/shard_map/all_gather | solution.py:21
  51.7 8.5 %copy-start = (bf16[192,2,2048]{2,1,0:T(2,128)(2,1)S(1)}, bf16[192,2,2048]{2,1,0:T(2,128)(2,1)}, u32[]{:S(2)}) copy-start(bf16[192,2,2048]{2,1,0:T(2,128)(2,1)} %param.3) | copy-start | bytes 4718596
  60.2 6.9 %collective-permute-start = (bf16[2,192,2,2048]{3,2,1,0:T(2,128)(2,1)}, bf16[2,192,2,2048]{3,2,1,0:T(2,128)(2,1)}, u32[]{:S(2)}, u32[]{:S(2)}) collective-permute-start(bf16[2,192,2,2048]{3,2,1,0:T(2,128)(2,1)} %pad_maximum_fusion), channel_id=1, source_target_pairs={{0,8},{8,0},{1,9},{9,1},{2,10},{10,2},{3,11},{11,3},{4,12},{12,4},... | collective-permute-start | bytes 9437192 | tf_op jit(solution)/shard_map/ppermute | solution.py:17
  65.4 1.7 copy-start.1
  184.5 3.7 %collective-permute-start.1 = (bf16[2,192,2,8,128]{4,3,2,1,0:T(8,128)(2,1)S(1)}, bf16[2,192,2,8,128]{4,3,2,1,0:T(8,128)(2,1)S(1)}, u32[]{:S(2)}, u32[]{:S(2)}) collective-permute-start(bf16[2,192,2,8,128]{4,3,2,1,0:T(8,128)(2,1)S(1)} %bitcast.54), channel_id=1, source_target_pairs={{0,8},{8,0},{1,9},{9,1},{2,10},{10,2},{3,11},{11,3},{4,12},{12,4},... | collective-permute-start | bytes 4718600 | tf_op jit(solution)/shard_map/ppermute | solution.py:33
Sparse Core Ops, SparseCore 0:
  10.2 41.4 all-gather.5
  54.0 108.9 all-gather.7

commit v3 on v2

v3 whole, which is shorter than its diff:
```python
import jax
import jax.numpy as jnp
from jax import lax
from jax.experimental import pallas as pl
from jax.experimental.pallas import tpu as pltpu
from jax.sharding import Mesh
from jax.sharding import PartitionSpec as P

SWAP = [(0, 1), (1, 0)]


def rotate_kernel(own_ref, partner_ref, ritz_ref, own_out, partner_out):
    rows = own_ref.shape[1]
    width = own_out.shape[-1]
    weights = ritz_ref[...].reshape(-1, 2 * width)
    for src, dst in ((own_ref, own_out), (partner_ref, partner_out)):
        lhs = src[...].reshape(2 * rows, -1)
        prod = jnp.dot(lhs, weights, preferred_element_type=jnp.float32)
        real = prod[:rows, :width] - prod[rows:, width:]
        imag = prod[:rows, width:] + prod[rows:, :width]
        dst[0] = real.astype(dst.dtype)
        dst[1] = imag.astype(dst.dtype)


def rotate(own, partner, gathered):
    q, rows, band = own.shape
    rc, cb, co, k, width2 = gathered.shape
    width = width2 // 2
    x_spec = pl.BlockSpec((q, rows, band), lambda c: (0, 0, 0))
    g_spec = pl.BlockSpec((rc, None, co, k, width2), lambda c: (0, c, 0, 0, 0))
    o_spec = pl.BlockSpec((2, None, rows, width), lambda c: (0, c, 0, 0))
    out = jax.ShapeDtypeStruct((2, cb, rows, width), jnp.bfloat16)
    flops = 2 * 2 * (2 * rows) * band * width2
    moved = 2 * own.size * 2 + gathered.size * 2 + 4 * rows * band * 2
    return pl.pallas_call(
        rotate_kernel,
        grid=(cb,),
        in_specs=[x_spec, x_spec, g_spec],
        out_specs=[o_spec, o_spec],
        out_shape=[out, out],
        compiler_params=pltpu.CompilerParams(vmem_limit_bytes=48 * 1024 * 1024),
        cost_estimate=pl.CostEstimate(flops=flops, transcendentals=0, bytes_accessed=moved),
    )(own, partner, gathered)


def shards(orbitals, applied_orbitals, ritz_matrix):
    me = lax.axis_index("core")
    rows = orbitals.shape[0]
    band_count = orbitals.shape[2]
    depth = ritz_matrix.shape[1]
    half = ritz_matrix.shape[2] // 2

    own = jnp.stack([orbitals, applied_orbitals]).transpose(2, 0, 1, 3).reshape(2, 2 * rows, band_count)
    partner = lax.ppermute(own, "core", SWAP)

    chip_block = lax.all_gather(ritz_matrix, "core")
    mine = lax.dynamic_slice_in_dim(chip_block, me * half, half, axis=3)
    mine = mine.transpose(0, 2, 1, 3).reshape(2, depth, 2 * half)
    gathered = lax.all_gather(lax.all_gather(mine, "col"), "rc")

    y_own, y_send = rotate(own, partner, gathered)
    recv = lax.ppermute(y_send, "core", SWAP)
    first = jnp.where(me == 0, y_own, recv)
    second = jnp.where(me == 0, recv, y_own)
    full = jnp.stack([first, second], 2)
    full = full.transpose(3, 0, 1, 2, 4).reshape(2, rows, 2, band_count)
    return full[0], full[1]


def solution(mesh):
    devices = mesh.devices
    split = Mesh(
        devices.reshape(devices.shape[0] // 2, 2, devices.shape[1]), ("rc", "core", "col")
    )
    flat = ("rc", "core", "col")
    in_specs = (P(flat, None, None), P(flat, None, None), P(None, ("rc", "core"), "col"))
    out_specs = (P(flat, None, None), P(flat, None, None))
    return jax.shard_map(shards, mesh=split, in_specs=in_specs, out_specs=out_specs, check_vma=False)
```

time: 206 us -> 202 us (0.981)
  matrix products: 19.2 us -> 0 us
  Pallas kernels: 0 us -> 17.8 us
  waiting for transfers between devices: 133 us -> 147 us
  local copies, waits for them, and re-layouts: 24.7 us -> 11.1 us
  other arithmetic: 10.9 us -> 8.03 us
    dot_general x1 -> x0, matrix products: 19.2 us -> none  [shards(): jnp.einsum('xanqrok,rcopkj->xanqpcj', lhs, gathered, preferred_element_ty...]
    pallas_call x0 -> x1, Pallas kernels: none -> 17.8 us  [rotate(): pl.pallas_call(rotate_kernel, grid=(cb,), in_specs=[x_spec, x_spec, g_spe...]
    another operation x5 -> x1, local copies, waits for them, and re-layouts: 12.1 us -> 0.74 us  [shards(): gathered = lax.all_gather(lax.all_gather(mine, 'col'), 'rc')]
    another operation x4 -> x1, other arithmetic: 9.95 us -> 1.61 us  [shards(): full = jnp.stack([first, second], 2)]
    all_gather x2, waiting for transfers between devices: 130 us -> 138 us  [shards(): gathered = lax.all_gather(lax.all_gather(mine, 'col'), 'rc')]
    transpose x0 -> x2, other arithmetic: none -> 6.41 us  [the longest x1 6.12 us: shards(): jnp.stack([orbitals, applied_orbitals]).transpose(2, 0, 1, 3)]
    ppermute x2, waiting for transfers between devices: 3.4 us -> 9.31 us  [the longest x1 5.79 us: shards(): partner = lax.ppermute(own, 'core', SWAP)]
    unnamed x9 -> x8, local copies, waits for them, and re-layouts: 10.9 us -> 8.66 us
  transfers between devices with their start and end apart: 4 -> 4, of which waited for: 3 -> 4; matrix products, arithmetic and copies ran while one was open for 10% -> 4% of each run, Pallas kernels for 0% -> 0%
where the time goes in v3:
time: 202 us; the launch traced here: 201 us
  waiting for transfers between devices  147 us (73%)
  Pallas kernels  17.8 us (9%)
  between operations  14.1 us (7%)
  local copies, waits for them, and re-layouts  11.1 us (5%)
  other arithmetic  8.03 us (4%)
  blocking collectives  2.34 us (1%)
    all_gather x2, waiting for transfers between devices, shards(): gathered = lax.all_gather(lax.all_gather(mine, 'col'), 'rc')  138 us
    pallas_call x1, Pallas kernels, rotate(): pl.pallas_call(rotate_kernel, grid=(cb,), in_specs=[x_spec, x_spec, g_spe...  17.8 us
    unnamed x8, local copies, waits for them, and re-layouts  8.66 us
    transpose x1, other arithmetic, shards(): jnp.stack([orbitals, applied_orbitals]).transpose(2, 0, 1, 3)  6.12 us
    ppermute x1, waiting for transfers between devices, shards(): partner = lax.ppermute(own, 'core', SWAP)  5.79 us
  transfers between devices with their start and end apart: 4, of which 4 were waited for; matrix products, arithmetic and copies ran while one was open for 4% of the time, Pallas kernels for 0%

profile of v3, /device:TPU:0, one launch (start us, length us, event | category | flops | bytes accessed | tf_op | source)
XLA Modules:
  0.0 200.9 jit_solution(14607286260022197952)
XLA Ops:
  7.2 0.0 copy-start.1
  7.2 0.0 all-gather.5.cloned.1.call-start
  7.2 2.3 %all-gather = bf16[4,128,256]{2,1,0:T(8,128)(2,1)S(1)} all-gather(bf16[2,128,256]{2,1,0:T(8,128)(2,1)} %param.5), channel_id=2, replica_groups=mesh['rc'=8,'core'=2,'col'=8] {'core'}, dimensions={0}, use_global_device_ids=true | all-gather | bytes 393216 | tf_op jit(solution)/shard_map/all_gather | solution.py:56
  9.6 0.1 copy.14
  9.7 0.7 all_gather_reshape.3
  10.5 0.0 all-gather.5.cloned.1.call-update
  10.5 0.0 all-gather.7.cloned.1.call-start
  10.6 41.5 %all-gather.5.cloned.1.call-done = bf16[8,2,128,256]{3,2,1,0:T(8,128)(2,1)} async-done(((bf16[1,2,128,256]{3,2,1,0:T(8,128)(2,1)}), bf16[8,2,128,256]{3,2,1,0:T(8,128)(2,1)}) %all-gather.5.cloned.1.call-update) | async-done | bytes 1048592 | tf_op jit(solution)/shard_map/all_gather | solution.py:59
  52.1 0.0 all-gather.7.cloned.1.call-update
  52.1 0.0 copy-done.1
  52.1 6.1 %maximum_bitcast_fusion = bf16[2,2,192,2048]{3,0,2,1:T(2,128)(2,1)S(1)} fusion(bf16[1,192,2,2048]{3,2,1,0:T(2,128)(2,1)S(1)} %bitcast.18, bf16[1,192,2,2048]{3,2,1,0:T(2,128)(2,1)} %bitcast.19), kind=kLoop, calls=%fused_computation | loop fusion | flops 1572864 | bytes 6291456 | tf_op jit(solution)/shard_map/transpose | solution.py:53
  58.2 1.4 copy.13
  59.6 0.0 copy-start
  59.6 1.7 copy-done
  61.3 0.0 collective-permute-start
  61.3 5.8 %collective-permute-done.partner_ref = bf16[2,384,2048]{2,1,0:T(8,128)(2,1)} collective-permute-done((bf16[2,384,2048]{2,1,0:T(8,128)(2,1)S(1)}, bf16[2,384,2048]{2,1,0:T(8,128)(2,1)}, u32[]{:S(2)}, u32[]{:S(2)}) %collective-permute-start) | collective-permute-done | bytes 3145760 | tf_op jit(solution)/shard_map/ppermute | solution.py:54
  67.1 96.2 %all-gather.7.cloned.1.call-done = bf16[64,2,128,256]{3,2,1,0:T(8,128)(2,1)} async-done(((bf16[8,2,128,256]{3,2,1,0:T(8,128)(2,1)}), bf16[64,2,128,256]{3,2,1,0:T(8,128)(2,1)}) %all-gather.7.cloned.1.call-update) | async-done | bytes 8388624 | tf_op jit(solution)/shard_map/all_gather | solution.py:59
  163.4 17.8 %shard_map.50 = (bf16[2,8,384,128]{3,2,1,0:T(8,128)(2,1)S(1)}, bf16[2,8,384,128]{3,2,1,0:T(8,128)(2,1)S(1)}) custom-call(bf16[2,384,2048]{2,1,0:T(8,128)(2,1)} %bitcast.16, bf16[2,384,2048]{2,1,0:T(8,128)(2,1)} %collective-permute-done.partner_ref, bf16[8,8,2,128,256]{4,3,2,1,0:T(8,128)(2,1)} %bitcast.17), custom_call_target="tpu_custom_call" | custom-call | flops 1610612736 | bytes 20971520 | tf_op jit(solution)/shard_map/pallas_call | solution.py:35
  181.2 0.3 collective-permute-start.1
  181.5 3.5 %collective-permute-done.1 = bf16[2,8,384,128]{3,2,1,0:T(8,128)(2,1)} collective-permute-done((bf16[2,8,384,128]{3,2,1,0:T(8,128)(2,1)S(1)}, bf16[2,8,384,128]{3,2,1,0:T(8,128)(2,1)}, u32[]{:S(2)}, u32[]{:S(2)}) %collective-permute-start.1) | collective-permute-done | bytes 1572896 | tf_op jit(solution)/shard_map/ppermute | solution.py:62
  185.0 1.6 select_bitcast_fusion.1
  186.6 0.3 maximum_bitcast_fusion.1
  186.9 0.2 fusion
  187.1 1.6 copy.20
  188.8 1.9 reshape.16
  190.6 1.6 copy.19
  192.2 1.9 reshape.15
  (1 shorter events, 0.0 us)
Async XLA Ops:
  7.2 45.0 %copy-start.1 = (bf16[192,2,2048]{2,1,0:T(2,128)(2,1)S(1)}, bf16[192,2,2048]{2,1,0:T(2,128)(2,1)}, u32[]{:S(2)}) copy-start(bf16[192,2,2048]{2,1,0:T(2,128)(2,1)} %param.4) | copy-start | bytes 4718596
  7.2 44.9 %all-gather.5.cloned.1.call-start = ((), (), s32[]{:S(2)}) async-start(), calls=%async_computation | async-start | bytes 1179648 | tf_op jit(solution)/shard_map/all_gather | solution.py:59
  10.5 152.9 %all-gather.7.cloned.1.call-start = ((), (), s32[]{:S(2)}) async-start(), calls=%async_computation.1 | async-start | bytes 9437184 | tf_op jit(solution)/shard_map/all_gather | solution.py:59
  59.6 1.7 copy-start
  61.3 5.8 %collective-permute-start = (bf16[2,384,2048]{2,1,0:T(8,128)(2,1)S(1)}, bf16[2,384,2048]{2,1,0:T(8,128)(2,1)}, u32[]{:S(2)}, u32[]{:S(2)}) collective-permute-start(bf16[2,384,2048]{2,1,0:T(8,128)(2,1)S(1)} %bitcast.15), channel_id=1, source_target_pairs={{0,8},{8,0},{1,9},{9,1},{2,10},{10,2},{3,11},{11,3},{4,12},{12,4},... | collective-permute-start | bytes 9437192 | tf_op jit(solution)/shard_map/ppermute | solution.py:54
  181.2 3.8 %collective-permute-start.1 = (bf16[2,8,384,128]{3,2,1,0:T(8,128)(2,1)S(1)}, bf16[2,8,384,128]{3,2,1,0:T(8,128)(2,1)}, u32[]{:S(2)}, u32[]{:S(2)}) collective-permute-start(bf16[2,8,384,128]{3,2,1,0:T(8,128)(2,1)S(1)} %get-tuple-element.5), channel_id=1, source_target_pairs={{0,8},{8,0},{1,9},{9,1},{2,10},{10,2},{3,11},{11,3},{4,12},{12,4},... | collective-permute-start | bytes 4718600 | tf_op jit(solution)/shard_map/ppermute | solution.py:62
Sparse Core Ops, SparseCore 0:
  10.6 41.4 all-gather.4
  54.4 108.9 all-gather.6

commit v4 on v3

--- a/solution.py
+++ b/solution.py
@@ -1,3 +1,5 @@
+import functools
+
 import jax
 import jax.numpy as jnp
 from jax import lax
@@ -7,6 +9,64 @@
 from jax.sharding import PartitionSpec as P
 
 SWAP = [(0, 1), (1, 0)]
+AXES = ("rc", "core", "col")
+MESH = pl.DeviceIdType.MESH
+
+
+def peer(axis, index):
+    ids = [lax.axis_index(a) for a in AXES]
+    ids[AXES.index(axis)] = index
+    return tuple(ids)
+
+
+def gather_kernel(axis, n, x_ref, out_ref, send_sem, recv_sem, local_sem):
+    me = lax.axis_index(axis)
+    barrier = pltpu.get_barrier_semaphore()
+    for d in range(1, n):
+        pl.semaphore_signal(barrier, 1, device_id=peer(axis, lax.rem(me + d, n)), device_id_type=MESH)
+    pl.semaphore_wait(barrier, n - 1)
+    local = pltpu.make_async_copy(x_ref, out_ref.at[me], local_sem)
+    local.start()
+    copies = []
+    for d in range(1, n):
+        copy = pltpu.make_async_remote_copy(
+            src_ref=x_ref,
+            dst_ref=out_ref.at[me],
+            send_sem=send_sem.at[d],
+            recv_sem=recv_sem.at[d],
+            device_id=peer(axis, lax.rem(me + d, n)),
+            device_id_type=MESH,
+        )
+        copy.start()
+        copies.append(copy)
+    for d, copy in enumerate(copies, 1):
+        copy.wait_send()
+        src = lax.rem(me + n - d, n)
+        incoming = pltpu.make_async_remote_copy(
+            src_ref=x_ref,
+            dst_ref=out_ref.at[src],
+            send_sem=send_sem.at[d],
+            recv_sem=recv_sem.at[d],
+            device_id=peer(axis, src),
+            device_id_type=MESH,
+        )
+        incoming.wait_recv()
+    local.wait()
+
+
+def gather(x, axis, n, cid):
+    return pl.pallas_call(
+        functools.partial(gather_kernel, axis, n),
+        out_shape=jax.ShapeDtypeStruct((n,) + x.shape, x.dtype),
+        in_specs=[pl.BlockSpec(memory_space=pl.ANY)],
+        out_specs=pl.BlockSpec(memory_space=pl.ANY),
+        scratch_shapes=[
+            pltpu.SemaphoreType.DMA((n,)),
+            pltpu.SemaphoreType.DMA((n,)),
+            pltpu.SemaphoreType.DMA(()),
+        ],
+        compiler_params=pltpu.CompilerParams(collective_id=cid, has_side_effects=True),
+    )(x)
 
 
 def rotate_kernel(own_ref, partner_ref, ritz_ref, own_out, partner_out):
@@ -43,7 +103,7 @@
     )(own, partner, gathered)
 
 
-def shards(orbitals, applied_orbitals, ritz_matrix):
+def shards(rc_count, col_count, orbitals, applied_orbitals, ritz_matrix):
     me = lax.axis_index("core")
     rows = orbitals.shape[0]
     band_count = orbitals.shape[2]
@@ -56,7 +116,7 @@
     chip_block = lax.all_gather(ritz_matrix, "core")
     mine = lax.dynamic_slice_in_dim(chip_block, me * half, half, axis=3)
     mine = mine.transpose(0, 2, 1, 3).reshape(2, depth, 2 * half)
-    gathered = lax.all_gather(lax.all_gather(mine, "col"), "rc")
+    gathered = gather(gather(mine, "col", col_count, 0), "rc", rc_count, 1)
 
     y_own, y_send = rotate(own, partner, gathered)
     recv = lax.ppermute(y_send, "core", SWAP)
@@ -75,4 +135,5 @@
     flat = ("rc", "core", "col")
     in_specs = (P(flat, None, None), P(flat, None, None), P(None, ("rc", "core"), "col"))
     out_specs = (P(flat, None, None), P(flat, None, None))
-    return jax.shard_map(shards, mesh=split, in_specs=in_specs, out_specs=out_specs, check_vma=False)
+    body = functools.partial(shards, devices.shape[0] // 2, devices.shape[1])
+    return jax.shard_map(body, mesh=split, in_specs=in_specs, out_specs=out_specs, check_vma=False)

time: 202 us -> 212 us (1.050)
  the two profiles are of different devices: /device:TPU:0 before, /device:TPU:117 now
where the time goes in v4:
time: 212 us
  Pallas kernels  181 us (85%)
  local copies, waits for them, and re-layouts  9.44 us (4%)
  other arithmetic  8.5 us (4%)
  blocking collectives  5.47 us (3%)
  waiting for transfers between devices  3.17 us (1%)
  starting transfers between devices  2.85 us (1%)
    pallas_call x2, Pallas kernels, gather(): pl.pallas_call(functools.partial(gather_kernel, axis, n), out_shape=jax.S...  164 us
    pallas_call x1, Pallas kernels, rotate(): pl.pallas_call(rotate_kernel, grid=(cb,), in_specs=[x_spec, x_spec, g_spe...  17.8 us
    unnamed x9, local copies, waits for them, and re-layouts  7.1 us
    transpose x1, other arithmetic, shards(): jnp.stack([orbitals, applied_orbitals]).transpose(2, 0, 1, 3)  6.59 us
    all_gather x1, blocking collectives, shards(): chip_block = lax.all_gather(ritz_matrix, 'core')  5.47 us
  transfers between devices with their start and end apart: 2, of which 1 were waited for; matrix products, arithmetic and copies ran while one was open for 0% of the time, Pallas kernels for 77%

profile of v4, /device:TPU:117, one launch (start us, length us, event | category | flops | bytes accessed | tf_op | source)
XLA Modules:
  0.0 211.6 jit_solution(16384275328229928498)
XLA Ops:
  0.6 6.6 %maximum_bitcast_fusion = bf16[2,2,192,2048]{3,0,2,1:T(2,128)(2,1)S(1)} fusion(bf16[1,192,2,2048]{3,2,1,0:T(2,128)(2,1)} %bitcast.17, bf16[1,192,2,2048]{3,2,1,0:T(2,128)(2,1)} %bitcast.18), kind=kLoop, calls=%fused_computation | loop fusion | flops 1572864 | bytes 6291456 | tf_op jit(solution)/shard_map/transpose | solution.py:113
  7.2 0.0 copy-start.1
  7.2 1.4 copy.13
  8.6 0.0 copy-start
  8.6 0.8 collective-permute-start
  9.4 0.0 copy-done.1
  9.4 5.5 %all-gather = bf16[4,128,256]{2,1,0:T(8,128)(2,1)S(1)} all-gather(bf16[2,128,256]{2,1,0:T(8,128)(2,1)S(1)} %copy-done.1), channel_id=2, replica_groups=mesh['rc'=8,'core'=2,'col'=8] {'core'}, dimensions={0}, use_global_device_ids=true | all-gather | bytes 393216 | tf_op jit(solution)/shard_map/all_gather | solution.py:116
  14.9 0.1 copy.25
  15.0 0.7 reshape.16.x_ref
  15.8 18.0 %shard_map.50.x_ref = bf16[8,2,128,256]{3,2,1,0:T(8,128)(2,1)} custom-call(bf16[2,128,256]{2,1,0:T(8,128)(2,1)} %reshape.16.x_ref), custom_call_target="tpu_custom_call" | custom-call | tf_op jit(solution)/shard_map/pallas_call | solution.py:58
  33.8 145.6 %shard_map.51.ritz_ref = bf16[8,8,2,128,256]{4,3,2,1,0:T(8,128)(2,1)} custom-call(bf16[8,2,128,256]{3,2,1,0:T(8,128)(2,1)} %shard_map.50.x_ref), custom_call_target="tpu_custom_call" | custom-call | tf_op jit(solution)/shard_map/pallas_call | solution.py:58
  179.4 0.0 copy-done
  179.4 0.0 collective-permute-done.partner_ref
  179.4 17.8 %shard_map.52 = (bf16[2,8,384,128]{3,2,1,0:T(8,128)(2,1)S(1)}, bf16[2,8,384,128]{3,2,1,0:T(8,128)(2,1)S(1)}) custom-call(bf16[2,384,2048]{2,1,0:T(8,128)(2,1)} %bitcast.16, bf16[2,384,2048]{2,1,0:T(8,128)(2,1)} %collective-permute-done.partner_ref, bf16[8,8,2,128,256]{4,3,2,1,0:T(8,128)(2,1)} %shard_map.51.ritz_ref), custom_call_target="tpu_custom_call" | custom-call | flops 1610612736 | bytes 20971520 | tf_op jit(solution)/shard_map/pallas_call | solution.py:95
  197.3 2.1 collective-permute-start.1
  199.3 3.2 %collective-permute-done.1 = bf16[2,8,384,128]{3,2,1,0:T(8,128)(2,1)} collective-permute-done((bf16[2,8,384,128]{3,2,1,0:T(8,128)(2,1)S(1)}, bf16[2,8,384,128]{3,2,1,0:T(8,128)(2,1)}, u32[]{:S(2)}, u32[]{:S(2)}) %collective-permute-start.1) | collective-permute-done | bytes 1572896 | tf_op jit(solution)/shard_map/ppermute | solution.py:122
  202.5 1.6 select_bitcast_fusion.1
  204.1 0.3 maximum_bitcast_fusion.1
  204.4 0.2 fusion
  204.6 1.6 copy.20
  206.3 1.9 reshape.19
  208.1 1.6 copy.19
  209.8 1.9 reshape.18
  (1 shorter events, 0.0 us)
Async XLA Ops:
  7.2 2.2 %copy-start.1 = (bf16[2,128,256]{2,1,0:T(8,128)(2,1)S(1)}, bf16[2,128,256]{2,1,0:T(8,128)(2,1)}, u32[]{:S(2)}) copy-start(bf16[2,128,256]{2,1,0:T(8,128)(2,1)} %param.5) | copy-start | bytes 393220
  8.6 170.8 %copy-start = (bf16[2,2,192,2048]{3,2,1,0:T(8,128)(2,1)}, bf16[2,2,192,2048]{3,2,1,0:T(8,128)(2,1)S(1)}, u32[]{:S(2)}) copy-start(bf16[2,2,192,2048]{3,2,1,0:T(8,128)(2,1)S(1)} %copy.13) | copy-start | bytes 9437188
  8.6 170.8 %collective-permute-start = (bf16[2,384,2048]{2,1,0:T(8,128)(2,1)S(1)}, bf16[2,384,2048]{2,1,0:T(8,128)(2,1)}, u32[]{:S(2)}, u32[]{:S(2)}) collective-permute-start(bf16[2,384,2048]{2,1,0:T(8,128)(2,1)S(1)} %bitcast.15), channel_id=1, source_target_pairs={{0,8},{8,0},{1,9},{9,1},{2,10},{10,2},{3,11},{11,3},{4,12},{12,4},... | collective-permute-start | bytes 9437192 | tf_op jit(solution)/shard_map/ppermute | solution.py:114
  197.3 5.3 %collective-permute-start.1 = (bf16[2,8,384,128]{3,2,1,0:T(8,128)(2,1)S(1)}, bf16[2,8,384,128]{3,2,1,0:T(8,128)(2,1)}, u32[]{:S(2)}, u32[]{:S(2)}) collective-permute-start(bf16[2,8,384,128]{3,2,1,0:T(8,128)(2,1)S(1)} %get-tuple-element.5), channel_id=1, source_target_pairs={{0,8},{8,0},{1,9},{9,1},{2,10},{10,2},{3,11},{11,3},{4,12},{12,4},... | collective-permute-start | bytes 4718600 | tf_op jit(solution)/shard_map/ppermute | solution.py:122

commit v5 on v4

--- a/solution.py
+++ b/solution.py
@@ -116,9 +116,15 @@
     chip_block = lax.all_gather(ritz_matrix, "core")
     mine = lax.dynamic_slice_in_dim(chip_block, me * half, half, axis=3)
     mine = mine.transpose(0, 2, 1, 3).reshape(2, depth, 2 * half)
-    gathered = gather(gather(mine, "col", col_count, 0), "rc", rc_count, 1)
+    strip = gather(mine, "col", col_count, 0)
+    split = (5 * col_count) // 8
+    offloaded = lax.all_gather(strip[:split], "rc")
+    direct = gather(strip[split:], "rc", rc_count, 1)
 
-    y_own, y_send = rotate(own, partner, gathered)
+    first_own, first_send = rotate(own, partner, offloaded)
+    second_own, second_send = rotate(own, partner, direct)
+    y_own = jnp.concatenate([first_own, second_own], 1)
+    y_send = jnp.concatenate([first_send, second_send], 1)
     recv = lax.ppermute(y_send, "core", SWAP)
     first = jnp.where(me == 0, y_own, recv)
     second = jnp.where(me == 0, recv, y_own)

time: 212 us -> 186 us (0.88)
  the two profiles are of different devices: /device:TPU:117 before, /device:TPU:0 now
where the time goes in v5:
time: 186 us; the launch traced here: 185 us
  Pallas kernels  96.8 us (52%)
  waiting for transfers between devices  48.2 us (26%)
  local copies, waits for them, and re-layouts  17.1 us (9%)
  between operations  14.2 us (8%)
  other arithmetic  6.49 us (3%)
  blocking collectives  2.21 us (1%)
    pallas_call x2, Pallas kernels, gather(): pl.pallas_call(functools.partial(gather_kernel, axis, n), out_shape=jax.S...  77.6 us
    all_gather x1, waiting for transfers between devices, shards(): offloaded = lax.all_gather(strip[:split], 'rc')  46.1 us
    pallas_call x2, Pallas kernels, rotate(): pl.pallas_call(rotate_kernel, grid=(cb,), in_specs=[x_spec, x_spec, g_spe...  19.2 us
    unnamed x20, local copies, waits for them, and re-layouts  10.9 us
    transpose x1, other arithmetic, shards(): jnp.stack([orbitals, applied_orbitals]).transpose(2, 0, 1, 3)  4.45 us
  transfers between devices with their start and end apart: 3, of which 2 were waited for; matrix products, arithmetic and copies ran while one was open for 5% of the time, Pallas kernels for 37%

profile of v5, /device:TPU:0, one launch (start us, length us, event | category | flops | bytes accessed | tf_op | source)
XLA Modules:
  0.0 185.0 jit_solution(10050035814638985403)
XLA Ops:
  7.2 0.0 all-gather.4.cloned.1.call-start
  7.2 2.2 %all-gather = bf16[4,128,256]{2,1,0:T(8,128)(2,1)S(1)} all-gather(bf16[2,128,256]{2,1,0:T(8,128)(2,1)} %param.5), channel_id=2, replica_groups=mesh['rc'=8,'core'=2,'col'=8] {'core'}, dimensions={0}, use_global_device_ids=true | all-gather | bytes 393216 | tf_op jit(solution)/shard_map/all_gather | solution.py:116
  9.4 0.1 copy.25
  9.6 0.7 reshape.16.x_ref
  10.3 0.0 copy-start.5
  10.3 0.0 copy-start.6
  10.3 17.7 %shard_map.50 = bf16[8,2,128,256]{3,2,1,0:T(8,128)(2,1)} custom-call(bf16[2,128,256]{2,1,0:T(8,128)(2,1)} %reshape.16.x_ref), custom_call_target="tpu_custom_call" | custom-call | tf_op jit(solution)/shard_map/pallas_call | solution.py:58
  28.0 2.0 %slice.14 = bf16[5,2,128,256]{3,2,1,0:T(8,128)(2,1)} slice(bf16[8,2,128,256]{3,2,1,0:T(8,128)(2,1)} %shard_map.50), slice={[0:5], [0:2], [0:128], [0:256]} | slice | bytes 1310720 | tf_op jit(solution)/shard_map/slice | solution.py:121
  30.0 0.0 all-gather.4.cloned.1.call-update
  30.0 0.0 copy-done.5
  30.0 0.0 copy-done.6
  30.0 4.4 %maximum_bitcast_fusion = bf16[2,2,192,2048]{3,0,2,1:T(2,128)(2,1)S(1)} fusion(bf16[1,192,2,2048]{3,2,1,0:T(2,128)(2,1)S(1)} %bitcast.20, bf16[1,192,2,2048]{3,2,1,0:T(2,128)(2,1)S(1)} %bitcast.21), kind=kLoop, calls=%fused_computation | loop fusion | flops 1572864 | bytes 6291456 | tf_op jit(solution)/shard_map/transpose | solution.py:113
  34.5 1.4 copy.13
  35.8 0.1 collective-permute-start
  35.9 1.8 slice.15.x_ref
  37.7 59.9 %shard_map.52.ritz_ref = bf16[8,3,2,128,256]{4,3,2,1,0:T(8,128)(2,1)} custom-call(bf16[3,2,128,256]{3,2,1,0:T(8,128)(2,1)} %slice.15.x_ref), custom_call_target="tpu_custom_call" | custom-call | tf_op jit(solution)/shard_map/pallas_call | solution.py:58
  97.7 0.0 collective-permute-done.partner_ref
  97.7 7.7 %shard_map.53 = (bf16[2,3,384,128]{3,2,1,0:T(8,128)(2,1)S(1)}, bf16[2,3,384,128]{3,2,1,0:T(8,128)(2,1)S(1)}) custom-call(bf16[2,384,2048]{2,1,0:T(8,128)(2,1)S(1)} %bitcast.17, bf16[2,384,2048]{2,1,0:T(8,128)(2,1)} %collective-permute-done.partner_ref, bf16[8,3,2,128,256]{4,3,2,1,0:T(8,128)(2,1)} %shard_map.52.ritz_ref), custom_call_target="tpu_custom_call" | custom-call | flops 1610612736 | bytes 15728640 | tf_op jit(solution)/shard_map/pallas_call | solution.py:95
  105.4 0.0 copy-start.1
  105.4 0.8 copy-done.1
  106.2 0.0 copy-start.3
  106.2 0.9 copy-done.3
  107.1 46.1 %all-gather.4.cloned.1.call-done = bf16[40,2,128,256]{3,2,1,0:T(8,128)(2,1)} async-done(((bf16[5,2,128,256]{3,2,1,0:T(8,128)(2,1)}), bf16[40,2,128,256]{3,2,1,0:T(8,128)(2,1)}) %all-gather.4.cloned.1.call-update) | async-done | bytes 5242896 | tf_op jit(solution)/shard_map/all_gather | solution.py:121
  153.2 0.0 copy-start.4
  153.2 11.4 %shard_map.51 = (bf16[2,5,384,128]{3,2,1,0:T(8,128)(2,1)S(1)}, bf16[2,5,384,128]{3,2,1,0:T(8,128)(2,1)S(1)}) custom-call(bf16[2,384,2048]{2,1,0:T(8,128)(2,1)S(1)} %bitcast.18, bf16[2,384,2048]{2,1,0:T(8,128)(2,1)} %collective-permute-done.partner_ref, bf16[8,5,2,128,256]{4,3,2,1,0:T(8,128)(2,1)} %bitcast.19), custom_call_target="tpu_custom_call" | custom-call | flops 1610612736 | bytes 17825792 | tf_op jit(solution)/shard_map/pallas_call | solution.py:95
  164.6 0.0 copy-start
  164.6 0.0 copy-done.4
  164.6 0.1 pad_maximum_fusion
  164.8 0.8 copy-done
  165.6 0.0 copy-start.2
  165.6 0.0 collective-permute-start.1
  165.6 1.3 constant_dynamic-update-slice_fusion.1
  166.9 0.0 copy-done.2
  166.9 0.1 constant_dynamic-update-slice_fusion
  167.0 2.1 %collective-permute-done.1 = bf16[2,8,384,128]{3,2,1,0:T(8,128)(2,1)} collective-permute-done((bf16[2,8,384,128]{3,2,1,0:T(8,128)(2,1)S(1)}, bf16[2,8,384,128]{3,2,1,0:T(8,128)(2,1)}, u32[]{:S(2)}, u32[]{:S(2)}) %collective-permute-start.1) | collective-permute-done | bytes 1572896 | tf_op jit(solution)/shard_map/ppermute | solution.py:128
  169.1 1.6 select_bitcast_fusion.1
  170.7 0.3 maximum_bitcast_fusion.1
  171.0 0.2 fusion
  171.2 1.6 copy.19
  172.9 1.9 %reshape.19 = bf16[192,2,2048]{2,1,0:T(2,128)(2,1)} reshape(bf16[192,2,8,2,128]{4,3,2,1,0:T(2,128)(2,1)S(1)} %copy.19) | data formatting | bytes 3145728
  174.7 1.6 copy.20
  176.3 1.9 %reshape.20 = bf16[192,2,2048]{2,1,0:T(2,128)(2,1)} reshape(bf16[192,2,8,2,128]{4,3,2,1,0:T(2,128)(2,1)S(1)} %copy.20) | data formatting | bytes 3145728
  (1 shorter events, 0.0 us)
Async XLA Ops:
  7.2 146.0 %all-gather.4.cloned.1.call-start = ((), (), s32[]{:S(2)}) async-start(), calls=%async_computation | async-start | bytes 5898240 | tf_op jit(solution)/shard_map/all_gather | solution.py:121
  10.3 19.7 %copy-start.5 = (bf16[192,2,2048]{2,1,0:T(2,128)(2,1)S(1)}, bf16[192,2,2048]{2,1,0:T(2,128)(2,1)}, u32[]{:S(2)}) copy-start(bf16[192,2,2048]{2,1,0:T(2,128)(2,1)} %param.4) | copy-start | bytes 4718596
  10.3 19.7 %copy-start.6 = (bf16[192,2,2048]{2,1,0:T(2,128)(2,1)S(1)}, bf16[192,2,2048]{2,1,0:T(2,128)(2,1)}, u32[]{:S(2)}) copy-start(bf16[192,2,2048]{2,1,0:T(2,128)(2,1)} %param.3) | copy-start | bytes 4718596
  35.8 61.8 %collective-permute-start = (bf16[2,384,2048]{2,1,0:T(8,128)(2,1)S(1)}, bf16[2,384,2048]{2,1,0:T(8,128)(2,1)}, u32[]{:S(2)}, u32[]{:S(2)}) collective-permute-start(bf16[2,384,2048]{2,1,0:T(8,128)(2,1)S(1)} %bitcast.16), channel_id=1, source_target_pairs={{0,8},{8,0},{1,9},{9,1},{2,10},{10,2},{3,11},{11,3},{4,12},{12,4},... | collective-permute-start | bytes 9437192 | tf_op jit(solution)/shard_map/ppermute | solution.py:114
  105.4 0.8 copy-start.1
  106.2 0.9 copy-start.3
  153.2 11.5 %copy-start.4 = (bf16[2,3,384,128]{3,2,1,0:T(8,128)(2,1)S(1)}, bf16[2,3,384,128]{3,2,1,0:T(8,128)(2,1)}, u32[]{:S(2)}) copy-start(bf16[2,3,384,128]{3,2,1,0:T(8,128)(2,1)} %copy-done.3) | copy-start | bytes 1769476
  164.6 0.9 copy-start
  165.6 1.4 copy-start.2
  165.6 3.5 %collective-permute-start.1 = (bf16[2,8,384,128]{3,2,1,0:T(8,128)(2,1)S(1)}, bf16[2,8,384,128]{3,2,1,0:T(8,128)(2,1)}, u32[]{:S(2)}, u32[]{:S(2)}) collective-permute-start(bf16[2,8,384,128]{3,2,1,0:T(8,128)(2,1)S(1)} %pad_maximum_fusion), channel_id=1, source_target_pairs={{0,8},{8,0},{1,9},{9,1},{2,10},{10,2},{3,11},{11,3},{4,12},{12,4},... | collective-permute-start | bytes 4718600 | tf_op jit(solution)/shard_map/ppermute | solution.py:128
Sparse Core Ops, SparseCore 0:
  30.1 122.9 all-gather.3

commit v6 on v3

--- a/solution.py
+++ b/solution.py
@@ -1,3 +1,5 @@
+import functools
+
 import jax
 import jax.numpy as jnp
 from jax import lax
@@ -7,6 +9,117 @@
 from jax.sharding import PartitionSpec as P
 
 SWAP = [(0, 1), (1, 0)]
+AXES = ("rc", "core", "col")
+MESH = pl.DeviceIdType.MESH
+
+
+RING = 4
+ORDERS = (("x", "y", "z"), ("y", "z", "x"))
+DIMS = ("y", "z_hi", "x", "z_lo")
+
+
+def ring_gather_kernel(x_ref, g_ref, send_sem, recv_sem, local_sem):
+    rc = lax.axis_index("rc")
+    core = lax.axis_index("core")
+    col = lax.axis_index("col")
+    here = {"y": rc // 2, "z": (rc % 2) * 2 + col % 2, "x": col // 2}
+
+    def device(axis, delta):
+        at = dict(here)
+        at[axis] = lax.rem(at[axis] + delta + RING, RING)
+        return (at["y"] * 2 + at["z"] // 2, core, at["x"] * 2 + at["z"] % 2)
+
+    def view(held, axis=None, delta=0, half=None):
+        at = dict(here)
+        if axis is not None:
+            at[axis] = lax.rem(at[axis] + delta + RING, RING)
+        index = []
+        split = half is not None
+        for dim in DIMS:
+            phys = "z" if dim.startswith("z") else dim
+            if phys in held:
+                size = 2 if phys == "z" else RING
+                if split:
+                    index.append(pl.ds(half * (size // 2), size // 2))
+                    split = False
+                else:
+                    index.append(slice(None))
+            elif dim == "z_hi":
+                index.append(at["z"] // 2)
+            elif dim == "z_lo":
+                index.append(at["z"] % 2)
+            else:
+                index.append(at[phys])
+        if split:
+            index.append(pl.ds(half, 1))
+        return g_ref.at[tuple(index)]
+
+    def remote(src, dst, slot, axis, delta):
+        return pltpu.make_async_remote_copy(
+            src_ref=src,
+            dst_ref=dst,
+            send_sem=send_sem.at[slot],
+            recv_sem=recv_sem.at[slot],
+            device_id=device(axis, delta),
+            device_id_type=MESH,
+        )
+
+    barrier = pltpu.get_barrier_semaphore()
+    for axis in ("x", "y", "z"):
+        for delta in (1, -1):
+            pl.semaphore_signal(barrier, 1, device_id=device(axis, delta), device_id_type=MESH)
+    pl.semaphore_wait(barrier, 6)
+
+    local = pltpu.make_async_copy(x_ref, view(()), local_sem)
+    local.start()
+
+    def run(order):
+        held = ()
+        for stage, axis in enumerate(order):
+            base = stage * 4
+            src = x_ref if stage == 0 else view(held)
+            out = [
+                remote(src, view(held), base + 0, axis, 1),
+                remote(src, view(held), base + 1, axis, -1),
+            ]
+            for copy in out:
+                copy.start()
+            remote(src, view(held, axis, -1), base + 0, axis, -1).wait_recv()
+            remote(src, view(held, axis, 1), base + 1, axis, 1).wait_recv()
+            fwd = [
+                remote(view(held, axis, 1, 0), view(held, axis, 1, 0), base + 2, axis, -1),
+                remote(view(held, axis, -1, 1), view(held, axis, -1, 1), base + 3, axis, 1),
+            ]
+            for copy in fwd:
+                copy.start()
+            remote(view(held, axis, 2, 0), view(held, axis, 2, 0), base + 2, axis, 1).wait_recv()
+            remote(view(held, axis, 2, 1), view(held, axis, 2, 1), base + 3, axis, -1).wait_recv()
+            for copy in out + fwd:
+                copy.wait_send()
+            if stage == 0:
+                local.wait()
+            held = held + (axis,)
+
+    for index, order in enumerate(ORDERS):
+        @pl.when(core == index)
+        def _():
+            run(order)
+
+
+def ring_gather(x):
+    shape = (RING, 2, RING, 2) + x.shape
+    return pl.pallas_call(
+        ring_gather_kernel,
+        out_shape=jax.ShapeDtypeStruct(shape, x.dtype),
+        in_specs=[pl.BlockSpec(memory_space=pl.ANY)],
+        out_specs=pl.BlockSpec(memory_space=pl.ANY),
+        scratch_shapes=[
+            pltpu.SemaphoreType.DMA((12,)),
+            pltpu.SemaphoreType.DMA((12,)),
+            pltpu.SemaphoreType.DMA(()),
+        ],
+        compiler_params=pltpu.CompilerParams(collective_id=0, has_side_effects=True),
+    )(x)
 
 
 def rotate_kernel(own_ref, partner_ref, ritz_ref, own_out, partner_out):
@@ -43,7 +156,7 @@
     )(own, partner, gathered)
 
 
-def shards(orbitals, applied_orbitals, ritz_matrix):
+def shards(rc_count, col_count, orbitals, applied_orbitals, ritz_matrix):
     me = lax.axis_index("core")
     rows = orbitals.shape[0]
     band_count = orbitals.shape[2]
@@ -56,8 +169,8 @@
     chip_block = lax.all_gather(ritz_matrix, "core")
     mine = lax.dynamic_slice_in_dim(chip_block, me * half, half, axis=3)
     mine = mine.transpose(0, 2, 1, 3).reshape(2, depth, 2 * half)
-    gathered = lax.all_gather(lax.all_gather(mine, "col"), "rc")
-
+    gathered = ring_gather(mine)
+    gathered = gathered.reshape((-1, gathered.shape[2] * gathered.shape[3]) + mine.shape)
     y_own, y_send = rotate(own, partner, gathered)
     recv = lax.ppermute(y_send, "core", SWAP)
     first = jnp.where(me == 0, y_own, recv)
@@ -75,4 +188,5 @@
     flat = ("rc", "core", "col")
     in_specs = (P(flat, None, None), P(flat, None, None), P(None, ("rc", "core"), "col"))
     out_specs = (P(flat, None, None), P(flat, None, None))
-    return jax.shard_map(shards, mesh=split, in_specs=in_specs, out_specs=out_specs, check_vma=False)
+    body = functools.partial(shards, devices.shape[0] // 2, devices.shape[1])
+    return jax.shard_map(body, mesh=split, in_specs=in_specs, out_specs=out_specs, check_vma=False)

time: 202 us -> 118 us (0.58)
  waiting for transfers between devices: 147 us -> 3.52 us
  Pallas kernels: 17.8 us -> 88.2 us
  between operations: 14.1 us -> 0.77 us
  blocking collectives: 2.34 us -> 5.82 us
    all_gather x2 -> x0, waiting for transfers between devices: 138 us -> none  [shards(): gathered = lax.all_gather(lax.all_gather(mine, 'col'), 'rc')]
    pallas_call x0 -> x1, Pallas kernels: none -> 70.3 us  [ring_gather(): pl.pallas_call(ring_gather_kernel, out_shape=jax.ShapeDtypeStruct(shape,...]
    ppermute x1, waiting for transfers between devices: 5.79 us -> 0.01 us  [shards(): partner = lax.ppermute(own, 'core', SWAP)]
    all_gather x1, blocking collectives: 2.34 us -> 5.82 us  [shards(): chip_block = lax.all_gather(ritz_matrix, 'core')]
    unnamed x8 -> x9, local copies, waits for them, and re-layouts: 8.66 us -> 7.1 us
  transfers between devices with their start and end apart: 4 -> 2, of which waited for: 4 -> 1; matrix products, arithmetic and copies ran while one was open for 4% -> 1% of each run, Pallas kernels for 0% -> 60%
where the time goes in v6:
time: 118 us; the launch traced here: 117 us
  Pallas kernels  88.2 us (75%)
  local copies, waits for them, and re-layouts  9.44 us (8%)
  other arithmetic  8.5 us (7%)
  blocking collectives  5.82 us (5%)
  waiting for transfers between devices  3.52 us (3%)
    pallas_call x1, Pallas kernels, ring_gather(): pl.pallas_call(ring_gather_kernel, out_shape=jax.ShapeDtypeStruct(shape,...  70.3 us
    pallas_call x1, Pallas kernels, rotate(): pl.pallas_call(rotate_kernel, grid=(cb,), in_specs=[x_spec, x_spec, g_spe...  17.9 us
    unnamed x9, local copies, waits for them, and re-layouts  7.1 us
    transpose x1, other arithmetic, shards(): jnp.stack([orbitals, applied_orbitals]).transpose(2, 0, 1, 3)  6.59 us
    all_gather x1, blocking collectives, shards(): chip_block = lax.all_gather(ritz_matrix, 'core')  5.82 us
    ppermute x1, waiting for transfers between devices, shards(): recv = lax.ppermute(y_send, 'core', SWAP)  3.52 us
  transfers between devices with their start and end apart: 2, of which 1 were waited for; matrix products, arithmetic and copies ran while one was open for 1% of the time, Pallas kernels for 60%

profile of v6, /device:TPU:0, one launch (start us, length us, event | category | flops | bytes accessed | tf_op | source)
XLA Modules:
  0.0 116.6 jit_solution(774103392097317615)
XLA Ops:
  0.6 6.6 %maximum_bitcast_fusion = bf16[2,2,192,2048]{3,0,2,1:T(2,128)(2,1)S(1)} fusion(bf16[1,192,2,2048]{3,2,1,0:T(2,128)(2,1)} %bitcast.19, bf16[1,192,2,2048]{3,2,1,0:T(2,128)(2,1)} %bitcast.20), kind=kLoop, calls=%fused_computation | loop fusion | flops 1572864 | bytes 6291456 | tf_op jit(solution)/shard_map/transpose | solution.py:166
  7.2 0.0 copy-start.1
  7.2 1.4 %copy.13 = bf16[2,2,192,2048]{3,2,1,0:T(8,128)(2,1)S(1)} copy(bf16[2,2,192,2048]{3,0,2,1:T(2,128)(2,1)S(1)} %maximum_bitcast_fusion) | data formatting | bytes 6291456 | tf_op jit(solution)/shard_map/transpose | solution.py:166
  8.6 0.0 copy-start
  8.6 0.1 collective-permute-start
  8.7 0.0 copy-done.1
  8.7 5.8 %all-gather = bf16[4,128,256]{2,1,0:T(8,128)(2,1)S(1)} all-gather(bf16[2,128,256]{2,1,0:T(8,128)(2,1)S(1)} %copy-done.1), channel_id=2, replica_groups=mesh['rc'=8,'core'=2,'col'=8] {'core'}, dimensions={0}, use_global_device_ids=true | all-gather | bytes 393216 | tf_op jit(solution)/shard_map/all_gather | solution.py:169
  14.6 0.1 copy.25
  14.7 0.7 reshape.19.x_ref
  15.5 70.3 %shard_map.50 = bf16[4,2,4,2,2,128,256]{6,5,4,3,2,1,0:T(8,128)(2,1)} custom-call(bf16[2,128,256]{2,1,0:T(8,128)(2,1)} %reshape.19.x_ref), custom_call_target="tpu_custom_call" | custom-call | tf_op jit(solution)/shard_map/pallas_call | solution.py:111
  85.8 0.0 copy-done
  85.8 0.0 collective-permute-done.partner_ref
  85.8 17.9 %shard_map.51 = (bf16[2,8,384,128]{3,2,1,0:T(8,128)(2,1)S(1)}, bf16[2,8,384,128]{3,2,1,0:T(8,128)(2,1)S(1)}) custom-call(bf16[2,384,2048]{2,1,0:T(8,128)(2,1)} %bitcast.18, bf16[2,384,2048]{2,1,0:T(8,128)(2,1)} %collective-permute-done.partner_ref, bf16[8,8,2,128,256]{4,3,2,1,0:T(8,128)(2,1)} %bitcast.16), custom_call_target="tpu_custom_call" | custom-call | flops 1610612736 | bytes 20971520 | tf_op jit(solution)/shard_map/pallas_call | solution.py:148
  103.7 0.3 collective-permute-start.1
  104.0 3.5 %collective-permute-done.1 = bf16[2,8,384,128]{3,2,1,0:T(8,128)(2,1)} collective-permute-done((bf16[2,8,384,128]{3,2,1,0:T(8,128)(2,1)S(1)}, bf16[2,8,384,128]{3,2,1,0:T(8,128)(2,1)}, u32[]{:S(2)}, u32[]{:S(2)}) %collective-permute-start.1) | collective-permute-done | bytes 1572896 | tf_op jit(solution)/shard_map/ppermute | solution.py:175
  107.5 1.6 %select_bitcast_fusion.1 = (bf16[2,8,1,384,128]{4,3,1,0,2:T(8,128)(2,1)S(1)}, bf16[2,8,1,384,128]{4,3,1,0,2:T(8,128)(2,1)S(1)}) fusion(bf16[2,8,384,128]{3,2,1,0:T(8,128)(2,1)S(1)} %get-tuple-element.4, bf16[2,8,384,128]{3,2,1,0:T(8,128)(2,1)} %collective-permute-done.1, pred[]{:T(512)S(6)} %eq.4), kind=kLoop, calls=%fused_computation.3 | loop fusion | flops 1572864 | bytes 6291457 | tf_op jit(solution)/shard_map/stack | solution.py:178
  109.1 0.3 maximum_bitcast_fusion.1
  109.4 0.2 fusion
  109.6 1.6 %copy.20 = bf16[192,2,8,2,128]{4,3,2,1,0:T(2,128)(2,1)S(1)} copy(bf16[192,2,8,2,128]{4,0,2,1,3:T(8,128)(2,1)S(1)} %get-tuple-element.10) | data formatting | bytes 3145728
  111.3 1.9 %reshape.23 = bf16[192,2,2048]{2,1,0:T(2,128)(2,1)} reshape(bf16[192,2,8,2,128]{4,3,2,1,0:T(2,128)(2,1)S(1)} %copy.20) | data formatting | bytes 3145728
  113.1 1.6 %copy.19 = bf16[192,2,8,2,128]{4,3,2,1,0:T(2,128)(2,1)S(1)} copy(bf16[192,2,8,2,128]{4,0,2,1,3:T(8,128)(2,1)S(1)} %get-tuple-element.11) | data formatting | bytes 3145728
  114.7 1.9 %reshape.22 = bf16[192,2,2048]{2,1,0:T(2,128)(2,1)} reshape(bf16[192,2,8,2,128]{4,3,2,1,0:T(2,128)(2,1)S(1)} %copy.19) | data formatting | bytes 3145728
  (1 shorter events, 0.0 us)
Async XLA Ops:
  7.2 1.5 %copy-start.1 = (bf16[2,128,256]{2,1,0:T(8,128)(2,1)S(1)}, bf16[2,128,256]{2,1,0:T(8,128)(2,1)}, u32[]{:S(2)}) copy-start(bf16[2,128,256]{2,1,0:T(8,128)(2,1)} %param.5) | copy-start | bytes 393220
  8.6 77.2 %copy-start = (bf16[2,2,192,2048]{3,2,1,0:T(8,128)(2,1)}, bf16[2,2,192,2048]{3,2,1,0:T(8,128)(2,1)S(1)}, u32[]{:S(2)}) copy-start(bf16[2,2,192,2048]{3,2,1,0:T(8,128)(2,1)S(1)} %copy.13) | copy-start | bytes 9437188
  8.6 77.2 %collective-permute-start = (bf16[2,384,2048]{2,1,0:T(8,128)(2,1)S(1)}, bf16[2,384,2048]{2,1,0:T(8,128)(2,1)}, u32[]{:S(2)}, u32[]{:S(2)}) collective-permute-start(bf16[2,384,2048]{2,1,0:T(8,128)(2,1)S(1)} %bitcast.17), channel_id=1, source_target_pairs={{0,8},{8,0},{1,9},{9,1},{2,10},{10,2},{3,11},{11,3},{4,12},{12,4},... | collective-permute-start | bytes 9437192 | tf_op jit(solution)/shard_map/ppermute | solution.py:167
  103.7 3.8 %collective-permute-start.1 = (bf16[2,8,384,128]{3,2,1,0:T(8,128)(2,1)S(1)}, bf16[2,8,384,128]{3,2,1,0:T(8,128)(2,1)}, u32[]{:S(2)}, u32[]{:S(2)}) collective-permute-start(bf16[2,8,384,128]{3,2,1,0:T(8,128)(2,1)S(1)} %get-tuple-element.5), channel_id=1, source_target_pairs={{0,8},{8,0},{1,9},{9,1},{2,10},{10,2},{3,11},{11,3},{4,12},{12,4},... | collective-permute-start | bytes 4718600 | tf_op jit(solution)/shard_map/ppermute | solution.py:175

commit v7 on v6

--- a/solution.py
+++ b/solution.py
@@ -64,20 +64,50 @@
             device_id_type=MESH,
         )
 
+    partner = (rc, 1 - core, col)
     barrier = pltpu.get_barrier_semaphore()
     for axis in ("x", "y", "z"):
         for delta in (1, -1):
             pl.semaphore_signal(barrier, 1, device_id=device(axis, delta), device_id_type=MESH)
-    pl.semaphore_wait(barrier, 6)
-
-    local = pltpu.make_async_copy(x_ref, view(()), local_sem)
-    local.start()
+    pl.semaphore_signal(barrier, 1, device_id=partner, device_id_type=MESH)
+    pl.semaphore_wait(barrier, 7)
+
+    width = x_ref.shape[2] // 2
+    unit = view(())
+    keep = pl.multiple_of(core * width, width)
+    give = pl.multiple_of((1 - core) * width, width)
+    moves = []
+    for p in range(2):
+        dst = unit.at[core, :, pl.ds(p * width, width)]
+        local = pltpu.make_async_copy(x_ref.at[p, :, pl.ds(keep, width)], dst, local_sem.at[p])
+        local.start()
+        swap = pltpu.make_async_remote_copy(
+            src_ref=x_ref.at[p, :, pl.ds(give, width)],
+            dst_ref=dst,
+            send_sem=send_sem.at[12 + p],
+            recv_sem=recv_sem.at[12 + p],
+            device_id=partner,
+            device_id_type=MESH,
+        )
+        swap.start()
+        moves.append((local, swap, unit.at[1 - core, :, pl.ds(p * width, width)], p))
+    for local, swap, dst, p in moves:
+        local.wait()
+        swap.wait_send()
+        pltpu.make_async_remote_copy(
+            src_ref=x_ref.at[p, :, pl.ds(give, width)],
+            dst_ref=dst,
+            send_sem=send_sem.at[12 + p],
+            recv_sem=recv_sem.at[12 + p],
+            device_id=partner,
+            device_id_type=MESH,
+        ).wait_recv()
 
     def run(order):
         held = ()
         for stage, axis in enumerate(order):
             base = stage * 4
-            src = x_ref if stage == 0 else view(held)
+            src = view(held)
             out = [
                 remote(src, view(held), base + 0, axis, 1),
                 remote(src, view(held), base + 1, axis, -1),
@@ -96,8 +126,6 @@
             remote(view(held, axis, 2, 1), view(held, axis, 2, 1), base + 3, axis, -1).wait_recv()
             for copy in out + fwd:
                 copy.wait_send()
-            if stage == 0:
-                local.wait()
             held = held + (axis,)
 
     for index, order in enumerate(ORDERS):
@@ -107,44 +135,44 @@
 
 
 def ring_gather(x):
-    shape = (RING, 2, RING, 2) + x.shape
+    shape = (RING, 2, RING, 2, 2, x.shape[1], x.shape[2])
     return pl.pallas_call(
         ring_gather_kernel,
         out_shape=jax.ShapeDtypeStruct(shape, x.dtype),
         in_specs=[pl.BlockSpec(memory_space=pl.ANY)],
         out_specs=pl.BlockSpec(memory_space=pl.ANY),
         scratch_shapes=[
-            pltpu.SemaphoreType.DMA((12,)),
-            pltpu.SemaphoreType.DMA((12,)),
-            pltpu.SemaphoreType.DMA(()),
+            pltpu.SemaphoreType.DMA((14,)),
+            pltpu.SemaphoreType.DMA((14,)),
+            pltpu.SemaphoreType.DMA((2,)),
         ],
         compiler_params=pltpu.CompilerParams(collective_id=0, has_side_effects=True),
     )(x)
 
 
 def rotate_kernel(own_ref, partner_ref, ritz_ref, own_out, partner_out):
-    rows = own_ref.shape[1]
+    band = own_ref.shape[1] // 2
     width = own_out.shape[-1]
     weights = ritz_ref[...].reshape(-1, 2 * width)
     for src, dst in ((own_ref, own_out), (partner_ref, partner_out)):
-        lhs = src[...].reshape(2 * rows, -1)
-        prod = jnp.dot(lhs, weights, preferred_element_type=jnp.float32)
-        real = prod[:rows, :width] - prod[rows:, width:]
-        imag = prod[:rows, width:] + prod[rows:, :width]
+        first = jnp.dot(src[:, :band], weights, preferred_element_type=jnp.float32)
+        second = jnp.dot(src[:, band:], weights, preferred_element_type=jnp.float32)
+        real = first[:, :width] - second[:, width:]
+        imag = first[:, width:] + second[:, :width]
         dst[0] = real.astype(dst.dtype)
         dst[1] = imag.astype(dst.dtype)
 
 
 def rotate(own, partner, gathered):
-    q, rows, band = own.shape
+    rows, band2 = own.shape
     rc, cb, co, k, width2 = gathered.shape
     width = width2 // 2
-    x_spec = pl.BlockSpec((q, rows, band), lambda c: (0, 0, 0))
+    x_spec = pl.BlockSpec((rows, band2), lambda c: (0, 0))
     g_spec = pl.BlockSpec((rc, None, co, k, width2), lambda c: (0, c, 0, 0, 0))
     o_spec = pl.BlockSpec((2, None, rows, width), lambda c: (0, c, 0, 0))
     out = jax.ShapeDtypeStruct((2, cb, rows, width), jnp.bfloat16)
-    flops = 2 * 2 * (2 * rows) * band * width2
-    moved = 2 * own.size * 2 + gathered.size * 2 + 4 * rows * band * 2
+    flops = 2 * 2 * rows * band2 * width2
+    moved = 2 * own.size * 2 + gathered.size * 2 + 2 * own.size * 2
     return pl.pallas_call(
         rotate_kernel,
         grid=(cb,),
@@ -160,23 +188,18 @@
     me = lax.axis_index("core")
     rows = orbitals.shape[0]
     band_count = orbitals.shape[2]
-    depth = ritz_matrix.shape[1]
-    half = ritz_matrix.shape[2] // 2
-
-    own = jnp.stack([orbitals, applied_orbitals]).transpose(2, 0, 1, 3).reshape(2, 2 * rows, band_count)
+
+    gathered = ring_gather(ritz_matrix)
+    gathered = gathered.reshape((-1, gathered.shape[2] * gathered.shape[3]) + gathered.shape[4:])
+    own = jnp.concatenate([orbitals.reshape(rows, -1), applied_orbitals.reshape(rows, -1)])
     partner = lax.ppermute(own, "core", SWAP)
-
-    chip_block = lax.all_gather(ritz_matrix, "core")
-    mine = lax.dynamic_slice_in_dim(chip_block, me * half, half, axis=3)
-    mine = mine.transpose(0, 2, 1, 3).reshape(2, depth, 2 * half)
-    gathered = ring_gather(mine)
-    gathered = gathered.reshape((-1, gathered.shape[2] * gathered.shape[3]) + mine.shape)
     y_own, y_send = rotate(own, partner, gathered)
     recv = lax.ppermute(y_send, "core", SWAP)
     first = jnp.where(me == 0, y_own, recv)
     second = jnp.where(me == 0, recv, y_own)
     full = jnp.stack([first, second], 2)
-    full = full.transpose(3, 0, 1, 2, 4).reshape(2, rows, 2, band_count)
+    full = full.reshape(2, -1, 2, 2, rows, full.shape[-1])
+    full = full.transpose(3, 4, 0, 1, 2, 5).reshape(2, rows, 2, band_count)
     return full[0], full[1]
 
 

time: 118 us -> 110 us (0.932)
  other arithmetic: 8.5 us -> 1.9 us
  blocking collectives: 5.82 us -> 0 us
  Pallas kernels: 88.2 us -> 91.4 us
  local copies, waits for them, and re-layouts: 9.44 us -> 11.4 us
    transpose x2 -> x1, other arithmetic: 6.88 us -> 0.29 us  [shards(): full = full.transpose(3, 4, 0, 1, 2, 5).reshape(2, rows, 2, band_count)]
    all_gather x1 -> x0, blocking collectives: 5.82 us -> none  [shards(): chip_block = lax.all_gather(ritz_matrix, 'core')]
    squeeze x0 -> x2, local copies, waits for them, and re-layouts: none -> 3.71 us  [shards(): return (full[0], full[1])]
    pallas_call x1, Pallas kernels: 70.3 us -> 73.6 us  [ring_gather(): pl.pallas_call(ring_gather_kernel, out_shape=jax.ShapeDtypeStruct(shape,...]
    slice x1 -> x3, local copies, waits for them, and re-layouts: 0.21 us -> 3.46 us  [shards(): return (full[0], full[1])]
    unnamed x9 -> x7, local copies, waits for them, and re-layouts: 7.1 us -> 4.1 us
    select_n x0 -> x1, other arithmetic: none -> 1.61 us  [shards(): first = jnp.where(me == 0, y_own, recv)]
    another operation x1 -> x0, other arithmetic: 1.61 us -> none  [shards(): full = jnp.stack([first, second], 2)]
  transfers between devices with their start and end apart: 2 -> 2, of which waited for: 1 -> 1; matrix products, arithmetic and copies ran while one was open for 1% -> 0% of each run, Pallas kernels for 60% -> 67%
where the time goes in v7:
time: 110 us; the launch traced here: 109 us
  Pallas kernels  91.4 us (83%)
  local copies, waits for them, and re-layouts  11.4 us (10%)
  waiting for transfers between devices  3.52 us (3%)
  other arithmetic  1.9 us (2%)
    pallas_call x1, Pallas kernels, ring_gather(): pl.pallas_call(ring_gather_kernel, out_shape=jax.ShapeDtypeStruct(shape,...  73.6 us
    pallas_call x1, Pallas kernels, rotate(): pl.pallas_call(rotate_kernel, grid=(cb,), in_specs=[x_spec, x_spec, g_spe...  17.8 us
    unnamed x7, local copies, waits for them, and re-layouts  4.1 us
    squeeze x2, local copies, waits for them, and re-layouts, shards(): return (full[0], full[1])  3.71 us
    ppermute x1, waiting for transfers between devices, shards(): recv = lax.ppermute(y_send, 'core', SWAP)  3.52 us
    slice x3, local copies, waits for them, and re-layouts, shards(): return (full[0], full[1])  3.46 us
  transfers between devices with their start and end apart: 2, of which 1 were waited for; matrix products, arithmetic and copies ran while one was open for 0% of the time, Pallas kernels for 67%

profile of v7, /device:TPU:0, one launch (start us, length us, event | category | flops | bytes accessed | tf_op | source)
XLA Modules:
  0.0 109.2 jit_solution(2278643044809627745)
XLA Ops:
  0.6 2.1 %copy.7 = bf16[24,8,2,2048]{3,1,2,0:T(8,128)(2,1)S(1)} copy(bf16[24,8,2,2048]{3,2,1,0:T(2,128)(2,1)} %bitcast.14) | data formatting | bytes 3145728
  2.7 0.0 copy-start.1
  2.7 0.1 constant_dynamic-update-slice_fusion.1
  2.8 1.2 %copy-done.1 = bf16[192,2,2048]{2,1,0:T(2,128)(2,1)S(1)} copy-done((bf16[192,2,2048]{2,1,0:T(2,128)(2,1)S(1)}, bf16[192,2,2048]{2,1,0:T(2,128)(2,1)}, u32[]{:S(2)}) %copy-start.1) | copy-done | bytes 1572888
  4.1 0.6 copy.8
  4.7 0.1 constant_dynamic-update-slice_fusion.own_ref
  4.9 0.0 copy-start
  4.9 0.1 collective-permute-start
  5.0 73.6 %shard_map.50 = bf16[4,2,4,2,2,128,256]{6,5,4,3,2,1,0:T(8,128)(2,1)} custom-call(bf16[2,128,256]{2,1,0:T(8,128)(2,1)} %x_ref.1), custom_call_target="tpu_custom_call" | custom-call | tf_op jit(solution)/shard_map/pallas_call | solution.py:139
  78.6 0.0 copy-done
  78.6 0.0 collective-permute-done.partner_ref
  78.7 17.8 %shard_map.51 = (bf16[2,8,384,128]{3,2,1,0:T(8,128)(2,1)S(1)}, bf16[2,8,384,128]{3,2,1,0:T(8,128)(2,1)S(1)}) custom-call(bf16[384,4096]{1,0:T(8,128)(2,1)} %copy-done, bf16[384,4096]{1,0:T(8,128)(2,1)} %collective-permute-done.partner_ref, bf16[8,8,2,128,256]{4,3,2,1,0:T(8,128)(2,1)} %bitcast.9), custom_call_target="tpu_custom_call" | custom-call | flops 1610612736 | bytes 20971520 | tf_op jit(solution)/shard_map/pallas_call | solution.py:176
  96.5 0.1 collective-permute-start.1
  96.6 3.5 %collective-permute-done.1 = bf16[2,8,384,128]{3,2,1,0:T(8,128)(2,1)} collective-permute-done((bf16[2,8,384,128]{3,2,1,0:T(8,128)(2,1)S(1)}, bf16[2,8,384,128]{3,2,1,0:T(8,128)(2,1)}, u32[]{:S(2)}, u32[]{:S(2)}) %collective-permute-start.1) | collective-permute-done | bytes 1572896 | tf_op jit(solution)/shard_map/ppermute | solution.py:197
  100.1 1.6 %broadcast_select_fusion.1 = (bf16[2,8,384,128]{3,2,1,0:T(8,128)(2,1)S(1)}, bf16[2,8,384,128]{3,2,1,0:T(8,128)(2,1)S(1)}) fusion(bf16[2,8,384,128]{3,2,1,0:T(8,128)(2,1)S(1)} %get-tuple-element.4, bf16[2,8,384,128]{3,2,1,0:T(8,128)(2,1)} %collective-permute-done.1, pred[]{:T(512)S(6)} %eq.4), kind=kLoop, calls=%fused_computation.2 | loop fusion | flops 1572864 | bytes 6291457 | tf_op jit(solution)/shard_map/jit(_where)/select_n | solution.py:198
  101.7 0.3 maximum_bitcast_fusion
  102.0 0.2 fusion
  102.2 1.6 %copy.5 = bf16[1,192,2,8,2,128]{5,4,3,2,1,0:T(2,128)(2,1)S(1)} copy(bf16[1,192,2,8,2,128]{5,1,0,3,2,4:T(8,128)(2,1)S(1)} %get-tuple-element.7) | data formatting | bytes 3145728 | tf_op jit(solution)/shard_map/slice | solution.py:203
  103.9 1.9 %squeeze.6 = bf16[192,2,2048]{2,1,0:T(2,128)(2,1)} reshape(bf16[1,192,2,8,2,128]{5,4,3,2,1,0:T(2,128)(2,1)S(1)} %copy.5) | data formatting | bytes 3145728 | tf_op jit(solution)/shard_map/squeeze | solution.py:203
  105.7 1.6 %copy.6 = bf16[1,192,2,8,2,128]{5,4,3,2,1,0:T(2,128)(2,1)S(1)} copy(bf16[1,192,2,8,2,128]{5,1,0,3,2,4:T(8,128)(2,1)S(1)} %get-tuple-element.6) | data formatting | bytes 3145728 | tf_op jit(solution)/shard_map/slice | solution.py:203
  107.3 1.9 %squeeze.7 = bf16[192,2,2048]{2,1,0:T(2,128)(2,1)} reshape(bf16[1,192,2,8,2,128]{5,4,3,2,1,0:T(2,128)(2,1)S(1)} %copy.6) | data formatting | bytes 3145728 | tf_op jit(solution)/shard_map/squeeze | solution.py:203
Async XLA Ops:
  2.7 1.4 %copy-start.1 = (bf16[192,2,2048]{2,1,0:T(2,128)(2,1)S(1)}, bf16[192,2,2048]{2,1,0:T(2,128)(2,1)}, u32[]{:S(2)}) copy-start(bf16[192,2,2048]{2,1,0:T(2,128)(2,1)} %param.4) | copy-start | bytes 4718596
  4.9 73.7 %copy-start = (bf16[384,4096]{1,0:T(8,128)(2,1)}, bf16[384,4096]{1,0:T(8,128)(2,1)S(1)}, u32[]{:S(2)}) copy-start(bf16[384,4096]{1,0:T(8,128)(2,1)S(1)} %constant_dynamic-update-slice_fusion.own_ref) | copy-start | bytes 9437188
  4.9 73.7 %collective-permute-start = (bf16[384,4096]{1,0:T(8,128)(2,1)S(1)}, bf16[384,4096]{1,0:T(8,128)(2,1)}, u32[]{:S(2)}, u32[]{:S(2)}) collective-permute-start(bf16[384,4096]{1,0:T(8,128)(2,1)S(1)} %constant_dynamic-update-slice_fusion.own_ref), channel_id=1, source_target_pairs={{0,8},{8,0},{1,9},{9,1},{2,10},{10,2},{3,11},{11,3},{4,12},{12,4},... | collective-permute-start | bytes 9437192 | tf_op jit(solution)/shard_map/ppermute | solution.py:195
  96.5 3.6 %collective-permute-start.1 = (bf16[2,8,384,128]{3,2,1,0:T(8,128)(2,1)S(1)}, bf16[2,8,384,128]{3,2,1,0:T(8,128)(2,1)}, u32[]{:S(2)}, u32[]{:S(2)}) collective-permute-start(bf16[2,8,384,128]{3,2,1,0:T(8,128)(2,1)S(1)} %get-tuple-element.5), channel_id=1, source_target_pairs={{0,8},{8,0},{1,9},{9,1},{2,10},{10,2},{3,11},{11,3},{4,12},{12,4},... | collective-permute-start | bytes 4718600 | tf_op jit(solution)/shard_map/ppermute | solution.py:197

commit v8 on v7

--- a/solution.py
+++ b/solution.py
@@ -18,7 +18,7 @@
 DIMS = ("y", "z_hi", "x", "z_lo")
 
 
-def ring_gather_kernel(x_ref, g_ref, send_sem, recv_sem, local_sem):
+def ring_rotate_kernel(x_ref, own_ref, own_out, send_out, g_ref, partner_ref, acc, send_sem, recv_sem, local_sem):
     rc = lax.axis_index("rc")
     core = lax.axis_index("core")
     col = lax.axis_index("col")
@@ -72,7 +72,48 @@
     pl.semaphore_signal(barrier, 1, device_id=partner, device_id_type=MESH)
     pl.semaphore_wait(barrier, 7)
 
+    acc[...] = jnp.zeros_like(acc)
+    lend = pltpu.make_async_remote_copy(
+        src_ref=own_ref,
+        dst_ref=partner_ref,
+        send_sem=send_sem.at[14],
+        recv_sem=recv_sem.at[14],
+        device_id=partner,
+        device_id_type=MESH,
+    )
+    lend.start()
+
+    band = own_ref.shape[1] // 2
     width = x_ref.shape[2] // 2
+    depth = 2 * x_ref.shape[1]
+
+    def compute(y, z, x):
+        w = g_ref[y, z // 2, x, z % 2].reshape(depth, 2 * width)
+        koff = pl.multiple_of((y * 2 + z // 2) * depth, depth)
+        block = x * 2 + z % 2
+        for src, rows in enumerate((own_ref, partner_ref)):
+            first = jnp.dot(rows[:, pl.ds(koff, depth)], w, preferred_element_type=jnp.float32)
+            second = jnp.dot(rows[:, pl.ds(band + koff, depth)], w, preferred_element_type=jnp.float32)
+            acc[src, 0, block] += first[:, :width] - second[:, width:]
+            acc[src, 1, block] += first[:, width:] + second[:, :width]
+
+    def compute_block(held, axis=None, delta=0):
+        at = dict(here)
+        if axis is not None:
+            at[axis] = lax.rem(at[axis] + delta + RING, RING)
+        full = [d for d in ("y", "z", "x") if d in held]
+
+        def body(i, carry):
+            c = dict(at)
+            rest = i
+            for d in full:
+                c[d] = rest % RING
+                rest = rest // RING
+            compute(c["y"], c["z"], c["x"])
+            return carry
+
+        lax.fori_loop(0, RING ** len(full), body, 0)
+
     unit = view(())
     keep = pl.multiple_of(core * width, width)
     give = pl.multiple_of((1 - core) * width, width)
@@ -114,6 +155,17 @@
             ]
             for copy in out:
                 copy.start()
+            if stage == 2:
+                lend.wait_send()
+                pltpu.make_async_remote_copy(
+                    src_ref=own_ref,
+                    dst_ref=partner_ref,
+                    send_sem=send_sem.at[14],
+                    recv_sem=recv_sem.at[14],
+                    device_id=partner,
+                    device_id_type=MESH,
+                ).wait_recv()
+                compute_block(held)
             remote(src, view(held, axis, -1), base + 0, axis, -1).wait_recv()
             remote(src, view(held, axis, 1), base + 1, axis, 1).wait_recv()
             fwd = [
@@ -122,10 +174,15 @@
             ]
             for copy in fwd:
                 copy.start()
+            if stage == 2:
+                compute_block(held, axis, -1)
+                compute_block(held, axis, 1)
             remote(view(held, axis, 2, 0), view(held, axis, 2, 0), base + 2, axis, 1).wait_recv()
             remote(view(held, axis, 2, 1), view(held, axis, 2, 1), base + 3, axis, -1).wait_recv()
             for copy in out + fwd:
                 copy.wait_send()
+            if stage == 2:
+                compute_block(held, axis, 2)
             held = held + (axis,)
 
     for index, order in enumerate(ORDERS):
@@ -133,21 +190,35 @@
         def _():
             run(order)
 
-
-def ring_gather(x):
-    shape = (RING, 2, RING, 2, 2, x.shape[1], x.shape[2])
+    own_out[...] = acc[0].astype(own_out.dtype)
+    send_out[...] = acc[1].astype(send_out.dtype)
+
+
+def ring_rotate(ritz, own):
+    rows, band2 = own.shape
+    units = (RING, 2, RING, 2, 2, ritz.shape[1], ritz.shape[2])
+    width = ritz.shape[2] // 2
+    out = jax.ShapeDtypeStruct((2, 2 * RING, rows, width), jnp.bfloat16)
+    vmem = pl.BlockSpec(memory_space=pltpu.VMEM)
+    flops = 2 * 2 * rows * band2 * 2 * ritz.shape[2] * 2 * RING
     return pl.pallas_call(
-        ring_gather_kernel,
-        out_shape=jax.ShapeDtypeStruct(shape, x.dtype),
-        in_specs=[pl.BlockSpec(memory_space=pl.ANY)],
-        out_specs=pl.BlockSpec(memory_space=pl.ANY),
+        ring_rotate_kernel,
+        out_shape=[out, out],
+        in_specs=[pl.BlockSpec(memory_space=pl.ANY), vmem],
+        out_specs=[vmem, vmem],
         scratch_shapes=[
-            pltpu.SemaphoreType.DMA((14,)),
-            pltpu.SemaphoreType.DMA((14,)),
+            pltpu.VMEM(units, ritz.dtype),
+            pltpu.VMEM((rows, band2), own.dtype),
+            pltpu.VMEM((2, 2, 2 * RING, rows, width), jnp.float32),
+            pltpu.SemaphoreType.DMA((15,)),
+            pltpu.SemaphoreType.DMA((15,)),
             pltpu.SemaphoreType.DMA((2,)),
         ],
-        compiler_params=pltpu.CompilerParams(collective_id=0, has_side_effects=True),
-    )(x)
+        compiler_params=pltpu.CompilerParams(
+            collective_id=0, has_side_effects=True, vmem_limit_bytes=60 * 1024 * 1024
+        ),
+        cost_estimate=pl.CostEstimate(flops=flops, transcendentals=0, bytes_accessed=4 * own.size * 2),
+    )(ritz, own)
 
 
 def rotate_kernel(own_ref, partner_ref, ritz_ref, own_out, partner_out):
@@ -189,11 +260,8 @@
     rows = orbitals.shape[0]
     band_count = orbitals.shape[2]
 
-    gathered = ring_gather(ritz_matrix)
-    gathered = gathered.reshape((-1, gathered.shape[2] * gathered.shape[3]) + gathered.shape[4:])
     own = jnp.concatenate([orbitals.reshape(rows, -1), applied_orbitals.reshape(rows, -1)])
-    partner = lax.ppermute(own, "core", SWAP)
-    y_own, y_send = rotate(own, partner, gathered)
+    y_own, y_send = ring_rotate(ritz_matrix, own)
     recv = lax.ppermute(y_send, "core", SWAP)
     first = jnp.where(me == 0, y_own, recv)
     second = jnp.where(me == 0, recv, y_own)

time: 110 us -> 99.5 us (0.905)
  Pallas kernels: 91.4 us -> 79.9 us
  other arithmetic: 1.9 us -> 3.9 us
  local copies, waits for them, and re-layouts: 11.4 us -> 9.98 us
    pallas_call x2 -> x1, Pallas kernels: 91.4 us -> 79.9 us  [ring_rotate(): pl.pallas_call(ring_rotate_kernel, out_shape=[out, out], in_specs=[pl.Blo...]
    concatenate x0 -> x1, other arithmetic: none -> 2 us  [shards(): jnp.concatenate([orbitals.reshape(rows, -1), applied_orbitals.reshape(row...]
    unnamed x7 -> x4, local copies, waits for them, and re-layouts: 4.1 us -> 2.82 us
  transfers between devices with their start and end apart: 2 -> 1, of which waited for: 1 -> 1; matrix products, arithmetic and copies ran while one was open for 0% -> 0% of each run, Pallas kernels for 67% -> 0%
where the time goes in v8:
time: 99.5 us; the launch traced here: 98.2 us
  Pallas kernels  79.9 us (80%)
  local copies, waits for them, and re-layouts  9.98 us (10%)
  other arithmetic  3.9 us (4%)
  waiting for transfers between devices  3.6 us (4%)
    pallas_call x1, Pallas kernels, ring_rotate(): pl.pallas_call(ring_rotate_kernel, out_shape=[out, out], in_specs=[pl.Blo...  79.9 us
    squeeze x2, local copies, waits for them, and re-layouts, shards(): return (full[0], full[1])  3.71 us
    ppermute x1, waiting for transfers between devices, shards(): recv = lax.ppermute(y_send, 'core', SWAP)  3.6 us
    slice x3, local copies, waits for them, and re-layouts, shards(): return (full[0], full[1])  3.45 us
    unnamed x4, local copies, waits for them, and re-layouts  2.82 us
    concatenate x1, other arithmetic, shards(): jnp.concatenate([orbitals.reshape(rows, -1), applied_orbitals.reshape(row...  2 us
  transfers between devices with their start and end apart: 1, of which 1 were waited for; matrix products, arithmetic and copies ran while one was open for 0% of the time, Pallas kernels for 0%

profile of v8, /device:TPU:0, one launch (start us, length us, event | category | flops | bytes accessed | tf_op | source)
XLA Modules:
  0.0 98.2 jit_solution(13599894864149272023)
XLA Ops:
  0.6 0.0 copy-start
  0.6 2.2 %copy.7 = bf16[24,8,2,2048]{3,1,2,0:T(8,128)(2,1)S(1)} copy(bf16[24,8,2,2048]{3,2,1,0:T(2,128)(2,1)} %bitcast.12) | data formatting | bytes 3145728
  2.8 0.0 copy-done
  2.8 0.6 copy.8
  3.5 2.0 %pad_maximum_fusion.own_ref = bf16[384,4096]{1,0:T(8,128)(2,1)} fusion(bf16[192,4096]{1,0:T(8,128)(2,1)S(1)} %bitcast.9, bf16[192,4096]{1,0:T(8,128)(2,1)S(1)} %bitcast.8), kind=kLoop, calls=%fused_computation | loop fusion | flops 6291456 | bytes 6291456 | tf_op jit(solution)/shard_map/concatenate | solution.py:263
  5.5 79.9 %shard_map.50 = (bf16[2,8,384,128]{3,2,1,0:T(8,128)(2,1)}, bf16[2,8,384,128]{3,2,1,0:T(8,128)(2,1)}) custom-call(bf16[2,128,256]{2,1,0:T(8,128)(2,1)} %x_ref.1, bf16[384,4096]{1,0:T(8,128)(2,1)} %pad_maximum_fusion.own_ref), custom_call_target="tpu_custom_call" | custom-call | flops 25769803776 | bytes 12582912 | tf_op jit(solution)/shard_map/pallas_call | solution.py:204
  85.4 0.1 collective-permute-start
  85.5 3.6 %collective-permute-done = bf16[2,8,384,128]{3,2,1,0:T(8,128)(2,1)S(1)} collective-permute-done((bf16[2,8,384,128]{3,2,1,0:T(8,128)(2,1)}, bf16[2,8,384,128]{3,2,1,0:T(8,128)(2,1)S(1)}, u32[]{:S(2)}, u32[]{:S(2)}) %collective-permute-start) | collective-permute-done | bytes 1572896 | tf_op jit(solution)/shard_map/ppermute | solution.py:265
  89.1 1.6 %broadcast_select_fusion.1 = (bf16[2,8,384,128]{3,2,1,0:T(8,128)(2,1)S(1)}, bf16[2,8,384,128]{3,2,1,0:T(8,128)(2,1)S(1)}) fusion(bf16[2,8,384,128]{3,2,1,0:T(8,128)(2,1)} %get-tuple-element.4, bf16[2,8,384,128]{3,2,1,0:T(8,128)(2,1)S(1)} %collective-permute-done, pred[]{:T(512)S(6)} %eq.4), kind=kLoop, calls=%fused_computation.3 | loop fusion | flops 1572864 | bytes 6291457 | tf_op jit(solution)/shard_map/jit(_where)/select_n | solution.py:266
  90.7 0.3 maximum_bitcast_fusion
  91.0 0.2 fusion
  91.3 1.6 %copy.6 = bf16[1,192,2,8,2,128]{5,4,3,2,1,0:T(2,128)(2,1)S(1)} copy(bf16[1,192,2,8,2,128]{5,1,0,3,2,4:T(8,128)(2,1)S(1)} %get-tuple-element.6) | data formatting | bytes 3145728 | tf_op jit(solution)/shard_map/slice | solution.py:271
  92.9 1.9 %squeeze.7 = bf16[192,2,2048]{2,1,0:T(2,128)(2,1)} reshape(bf16[1,192,2,8,2,128]{5,4,3,2,1,0:T(2,128)(2,1)S(1)} %copy.6) | data formatting | bytes 3145728 | tf_op jit(solution)/shard_map/squeeze | solution.py:271
  94.7 1.6 %copy.5 = bf16[1,192,2,8,2,128]{5,4,3,2,1,0:T(2,128)(2,1)S(1)} copy(bf16[1,192,2,8,2,128]{5,1,0,3,2,4:T(8,128)(2,1)S(1)} %get-tuple-element.7) | data formatting | bytes 3145728 | tf_op jit(solution)/shard_map/slice | solution.py:271
  96.4 1.9 %squeeze.6 = bf16[192,2,2048]{2,1,0:T(2,128)(2,1)} reshape(bf16[1,192,2,8,2,128]{5,4,3,2,1,0:T(2,128)(2,1)S(1)} %copy.5) | data formatting | bytes 3145728 | tf_op jit(solution)/shard_map/squeeze | solution.py:271
Async XLA Ops:
  0.6 2.2 %copy-start = (bf16[192,2,2048]{2,1,0:T(2,128)(2,1)S(1)}, bf16[192,2,2048]{2,1,0:T(2,128)(2,1)}, u32[]{:S(2)}) copy-start(bf16[192,2,2048]{2,1,0:T(2,128)(2,1)} %param.4) | copy-start | bytes 4718596
  85.4 3.7 %collective-permute-start = (bf16[2,8,384,128]{3,2,1,0:T(8,128)(2,1)}, bf16[2,8,384,128]{3,2,1,0:T(8,128)(2,1)S(1)}, u32[]{:S(2)}, u32[]{:S(2)}) collective-permute-start(bf16[2,8,384,128]{3,2,1,0:T(8,128)(2,1)} %get-tuple-element.5), channel_id=1, source_target_pairs={{0,8},{8,0},{1,9},{9,1},{2,10},{10,2},{3,11},{11,3},{4,12},{12,4},... | collective-permute-start | bytes 4718600 | tf_op jit(solution)/shard_map/ppermute | solution.py:265

commit v9 on v8

--- a/solution.py
+++ b/solution.py
@@ -18,7 +18,9 @@
 DIMS = ("y", "z_hi", "x", "z_lo")
 
 
-def ring_rotate_kernel(x_ref, own_ref, own_out, send_out, g_ref, partner_ref, acc, send_sem, recv_sem, local_sem):
+def ring_rotate_kernel(
+    x_ref, own_ref, orb_out, app_out, g_ref, partner_ref, acc, lent, back, send_sem, recv_sem, local_sem
+):
     rc = lax.axis_index("rc")
     core = lax.axis_index("core")
     col = lax.axis_index("col")
@@ -190,15 +192,44 @@
         def _():
             run(order)
 
-    own_out[...] = acc[0].astype(own_out.dtype)
-    send_out[...] = acc[1].astype(send_out.dtype)
+    lent[...] = acc[1].astype(lent.dtype)
+    give_back = pltpu.make_async_remote_copy(
+        src_ref=lent,
+        dst_ref=back,
+        send_sem=send_sem.at[15],
+        recv_sem=recv_sem.at[15],
+        device_id=partner,
+        device_id_type=MESH,
+    )
+    give_back.start()
+    rows = orb_out.shape[0]
+    blocks = acc.shape[2]
+
+    def store(values, h):
+        for a, out in enumerate((orb_out, app_out)):
+            for c in range(blocks):
+                lane = pl.multiple_of(c * 2 * width + h * width, width)
+                part = [values[p, c, pl.ds(a * rows, rows), :].astype(out.dtype) for p in range(2)]
+                out[:, :, pl.ds(lane, width)] = jnp.stack(part, axis=1)
+
+    store(acc.at[0], core)
+    give_back.wait_send()
+    pltpu.make_async_remote_copy(
+        src_ref=lent,
+        dst_ref=back,
+        send_sem=send_sem.at[15],
+        recv_sem=recv_sem.at[15],
+        device_id=partner,
+        device_id_type=MESH,
+    ).wait_recv()
+    store(back, 1 - core)
 
 
 def ring_rotate(ritz, own):
     rows, band2 = own.shape
     units = (RING, 2, RING, 2, 2, ritz.shape[1], ritz.shape[2])
     width = ritz.shape[2] // 2
-    out = jax.ShapeDtypeStruct((2, 2 * RING, rows, width), jnp.bfloat16)
+    out = jax.ShapeDtypeStruct((rows // 2, 2, band2 // 2), jnp.bfloat16)
     vmem = pl.BlockSpec(memory_space=pltpu.VMEM)
     flops = 2 * 2 * rows * band2 * 2 * ritz.shape[2] * 2 * RING
     return pl.pallas_call(
@@ -210,8 +241,10 @@
             pltpu.VMEM(units, ritz.dtype),
             pltpu.VMEM((rows, band2), own.dtype),
             pltpu.VMEM((2, 2, 2 * RING, rows, width), jnp.float32),
-            pltpu.SemaphoreType.DMA((15,)),
-            pltpu.SemaphoreType.DMA((15,)),
+            pltpu.VMEM((2, 2 * RING, rows, width), jnp.bfloat16),
+            pltpu.VMEM((2, 2 * RING, rows, width), jnp.bfloat16),
+            pltpu.SemaphoreType.DMA((16,)),
+            pltpu.SemaphoreType.DMA((16,)),
             pltpu.SemaphoreType.DMA((2,)),
         ],
         compiler_params=pltpu.CompilerParams(
@@ -261,14 +294,8 @@
     band_count = orbitals.shape[2]
 
     own = jnp.concatenate([orbitals.reshape(rows, -1), applied_orbitals.reshape(rows, -1)])
-    y_own, y_send = ring_rotate(ritz_matrix, own)
-    recv = lax.ppermute(y_send, "core", SWAP)
-    first = jnp.where(me == 0, y_own, recv)
-    second = jnp.where(me == 0, recv, y_own)
-    full = jnp.stack([first, second], 2)
-    full = full.reshape(2, -1, 2, 2, rows, full.shape[-1])
-    full = full.transpose(3, 4, 0, 1, 2, 5).reshape(2, rows, 2, band_count)
-    return full[0], full[1]
+    orb_out, app_out = ring_rotate(ritz_matrix, own)
+    return orb_out, app_out
 
 
 def solution(mesh):

time: 99.5 us -> 97.8 us (0.983)
  Pallas kernels: 79.9 us -> 86 us
  waiting for transfers between devices: 3.6 us -> 0 us
  local copies, waits for them, and re-layouts: 9.98 us -> 7.72 us
  other arithmetic: 3.9 us -> 2.01 us
    pallas_call x1, Pallas kernels: 79.9 us -> 86 us  [ring_rotate(): pl.pallas_call(ring_rotate_kernel, out_shape=[out, out], in_specs=[pl.Blo...]
    unnamed x4 -> x8, local copies, waits for them, and re-layouts: 2.82 us -> 7.72 us
    squeeze x2 -> x0, local copies, waits for them, and re-layouts: 3.71 us -> none  [shards(): return (full[0], full[1])]
    ppermute x1 -> x0, waiting for transfers between devices: 3.6 us -> none  [shards(): recv = lax.ppermute(y_send, 'core', SWAP)]
    slice x3 -> x0, local copies, waits for them, and re-layouts: 3.45 us -> none  [shards(): return (full[0], full[1])]
    select_n x1 -> x0, other arithmetic: 1.61 us -> none  [shards(): first = jnp.where(me == 0, y_own, recv)]
  transfers between devices with their start and end apart: 1 -> 0, of which waited for: 1 -> 0; matrix products, arithmetic and copies ran while one was open for 0% -> 0% of each run, Pallas kernels for 0% -> 0%
where the time goes in v9:
time: 97.8 us; the launch traced here: 96.4 us
  Pallas kernels  86 us (88%)
  local copies, waits for them, and re-layouts  7.72 us (8%)
  other arithmetic  2.01 us (2%)
    pallas_call x1, Pallas kernels, ring_rotate(): pl.pallas_call(ring_rotate_kernel, out_shape=[out, out], in_specs=[pl.Blo...  86 us
    unnamed x8, local copies, waits for them, and re-layouts  7.72 us
    concatenate x1, other arithmetic, shards(): jnp.concatenate([orbitals.reshape(rows, -1), applied_orbitals.reshape(row...  2.01 us

profile of v9, /device:TPU:0, one launch (start us, length us, event | category | flops | bytes accessed | tf_op | source)
XLA Modules:
  0.0 96.4 jit_solution(908031956289954790)
XLA Ops:
  0.6 0.0 copy-start
  0.6 2.2 %copy.5 = bf16[24,8,2,2048]{3,1,2,0:T(8,128)(2,1)S(1)} copy(bf16[24,8,2,2048]{3,2,1,0:T(2,128)(2,1)} %bitcast.6) | data formatting | bytes 3145728
  2.8 0.0 copy-done
  2.8 0.6 copy.6
  3.5 2.0 %pad_maximum_fusion.own_ref = bf16[384,4096]{1,0:T(8,128)(2,1)} fusion(bf16[192,4096]{1,0:T(8,128)(2,1)S(1)} %bitcast.5, bf16[192,4096]{1,0:T(8,128)(2,1)S(1)} %bitcast.4), kind=kLoop, calls=%fused_computation | loop fusion | flops 6291456 | bytes 6291456 | tf_op jit(solution)/shard_map/concatenate | solution.py:296
  5.5 86.0 %shard_map.50 = (bf16[192,2,2048]{2,1,0:T(2,128)(2,1)}, bf16[192,2,2048]{2,1,0:T(2,128)(2,1)}) custom-call(bf16[2,128,256]{2,1,0:T(8,128)(2,1)} %x_ref.1, bf16[384,4096]{1,0:T(8,128)(2,1)} %pad_maximum_fusion.own_ref), custom_call_target="tpu_custom_call" | custom-call | flops 25769803776 | bytes 12582912 | tf_op jit(solution)/shard_map/pallas_call | solution.py:235
  91.5 0.0 copy-start.1
  91.5 3.7 %copy.9 = bf16[192,2,2048]{2,1,0:T(2,128)(2,1)} copy(bf16[192,2,2048]{2,1,0:T(2,128)(2,1)} %get-tuple-element.4) | data formatting | bytes 3145728
  95.3 0.0 copy-done.1
  95.3 1.1 %copy.10 = bf16[192,2,2048]{2,1,0:T(2,128)(2,1)} copy(bf16[192,2,2048]{2,1,0:T(2,128)(2,1)S(1)} %copy-done.1) | data formatting | bytes 3145728
Async XLA Ops:
  0.6 2.2 %copy-start = (bf16[192,2,2048]{2,1,0:T(2,128)(2,1)S(1)}, bf16[192,2,2048]{2,1,0:T(2,128)(2,1)}, u32[]{:S(2)}) copy-start(bf16[192,2,2048]{2,1,0:T(2,128)(2,1)} %param.4) | copy-start | bytes 4718596
  91.5 3.8 %copy-start.1 = (bf16[192,2,2048]{2,1,0:T(2,128)(2,1)S(1)}, bf16[192,2,2048]{2,1,0:T(2,128)(2,1)}, u32[]{:S(2)}) copy-start(bf16[192,2,2048]{2,1,0:T(2,128)(2,1)} %get-tuple-element.5) | copy-start | bytes 4718596

commit v10 on v9

--- a/solution.py
+++ b/solution.py
@@ -19,7 +19,8 @@
 
 
 def ring_rotate_kernel(
-    x_ref, own_ref, orb_out, app_out, g_ref, partner_ref, acc, lent, back, send_sem, recv_sem, local_sem
+    x_ref, orb_ref, app_ref, orb_out, app_out, g_ref, own_ref, partner_ref, acc, lent, back, send_sem, recv_sem,
+    local_sem,
 ):
     rc = lax.axis_index("rc")
     core = lax.axis_index("core")
@@ -74,7 +75,6 @@
     pl.semaphore_signal(barrier, 1, device_id=partner, device_id_type=MESH)
     pl.semaphore_wait(barrier, 7)
 
-    acc[...] = jnp.zeros_like(acc)
     lend = pltpu.make_async_remote_copy(
         src_ref=own_ref,
         dst_ref=partner_ref,
@@ -83,7 +83,15 @@
         device_id=partner,
         device_id_type=MESH,
     )
-    lend.start()
+
+    def build():
+        count = orb_ref.shape[0]
+        step = 32
+        for a, raw in enumerate((orb_ref, app_ref)):
+            for n in range(0, count, step):
+                v = raw[pl.ds(n, step)]
+                for q in range(2):
+                    own_ref[pl.ds(a * count + n, step), pl.ds(q * band, band)] = v[:, q, :]
 
     band = own_ref.shape[1] // 2
     width = x_ref.shape[2] // 2
@@ -157,6 +165,10 @@
             ]
             for copy in out:
                 copy.start()
+            if stage == 0:
+                build()
+            if stage == 1:
+                acc[...] = jnp.zeros_like(acc)
             if stage == 2:
                 lend.wait_send()
                 pltpu.make_async_remote_copy(
@@ -183,6 +195,8 @@
             remote(view(held, axis, 2, 1), view(held, axis, 2, 1), base + 3, axis, -1).wait_recv()
             for copy in out + fwd:
                 copy.wait_send()
+            if stage == 0:
+                lend.start()
             if stage == 2:
                 compute_block(held, axis, 2)
             held = held + (axis,)
@@ -225,8 +239,9 @@
     store(back, 1 - core)
 
 
-def ring_rotate(ritz, own):
-    rows, band2 = own.shape
+def ring_rotate(ritz, orbitals, applied_orbitals):
+    rows, band2 = 2 * orbitals.shape[0], 2 * orbitals.shape[2]
+    own = orbitals
     units = (RING, 2, RING, 2, 2, ritz.shape[1], ritz.shape[2])
     width = ritz.shape[2] // 2
     out = jax.ShapeDtypeStruct((rows // 2, 2, band2 // 2), jnp.bfloat16)
@@ -235,10 +250,11 @@
     return pl.pallas_call(
         ring_rotate_kernel,
         out_shape=[out, out],
-        in_specs=[pl.BlockSpec(memory_space=pl.ANY), vmem],
+        in_specs=[pl.BlockSpec(memory_space=pl.ANY), vmem, vmem],
         out_specs=[vmem, vmem],
         scratch_shapes=[
             pltpu.VMEM(units, ritz.dtype),
+            pltpu.VMEM((rows, band2), own.dtype),
             pltpu.VMEM((rows, band2), own.dtype),
             pltpu.VMEM((2, 2, 2 * RING, rows, width), jnp.float32),
             pltpu.VMEM((2, 2 * RING, rows, width), jnp.bfloat16),
@@ -250,8 +266,8 @@
         compiler_params=pltpu.CompilerParams(
             collective_id=0, has_side_effects=True, vmem_limit_bytes=60 * 1024 * 1024
         ),
-        cost_estimate=pl.CostEstimate(flops=flops, transcendentals=0, bytes_accessed=4 * own.size * 2),
-    )(ritz, own)
+        cost_estimate=pl.CostEstimate(flops=flops, transcendentals=0, bytes_accessed=8 * own.size * 2),
+    )(ritz, orbitals, applied_orbitals)
 
 
 def rotate_kernel(own_ref, partner_ref, ritz_ref, own_out, partner_out):
@@ -293,8 +309,7 @@
     rows = orbitals.shape[0]
     band_count = orbitals.shape[2]
 
-    own = jnp.concatenate([orbitals.reshape(rows, -1), applied_orbitals.reshape(rows, -1)])
-    orb_out, app_out = ring_rotate(ritz_matrix, own)
+    orb_out, app_out = ring_rotate(ritz_matrix, orbitals, applied_orbitals)
     return orb_out, app_out
 
 

time: 97.8 us -> 95.1 us (0.972)
  local copies, waits for them, and re-layouts: 7.72 us -> 4.89 us
  Pallas kernels: 86 us -> 88.2 us
  other arithmetic: 2.01 us -> 0 us
    unnamed x8 -> x4, local copies, waits for them, and re-layouts: 7.72 us -> 4.89 us
    pallas_call x1, Pallas kernels: 86 us -> 88.2 us  [ring_rotate(): pl.pallas_call(ring_rotate_kernel, out_shape=[out, out], in_specs=[pl.Blo...]
    concatenate x1 -> x0, other arithmetic: 2.01 us -> none  [shards(): jnp.concatenate([orbitals.reshape(rows, -1), applied_orbitals.reshape(row...]
where the time goes in v10:
time: 95.1 us; the launch traced here: 93.7 us
  Pallas kernels  88.2 us (93%)
  local copies, waits for them, and re-layouts  4.89 us (5%)
    pallas_call x1, Pallas kernels, ring_rotate(): pl.pallas_call(ring_rotate_kernel, out_shape=[out, out], in_specs=[pl.Blo...  88.2 us
    unnamed x4, local copies, waits for them, and re-layouts  4.89 us

profile of v10, /device:TPU:0, one launch (start us, length us, event | category | flops | bytes accessed | tf_op | source)
XLA Modules:
  0.0 93.7 jit_solution(6676582450309564839)
XLA Ops:
  0.6 88.2 %shard_map.50 = (bf16[192,2,2048]{2,1,0:T(2,128)(2,1)}, bf16[192,2,2048]{2,1,0:T(2,128)(2,1)}) custom-call(bf16[2,128,256]{2,1,0:T(8,128)(2,1)} %x_ref.1, bf16[192,2,2048]{2,1,0:T(2,128)(2,1)} %orb_ref.1, bf16[192,2,2048]{2,1,0:T(2,128)(2,1)} %app_ref.1), custom_call_target="tpu_custom_call" | custom-call | flops 25769803776 | bytes 12582912 | tf_op jit(solution)/shard_map/pallas_call | solution.py:250
  88.8 0.0 copy-start
  88.8 3.7 %copy.7 = bf16[192,2,2048]{2,1,0:T(2,128)(2,1)} copy(bf16[192,2,2048]{2,1,0:T(2,128)(2,1)} %get-tuple-element.4) | data formatting | bytes 3145728
  92.6 0.0 copy-done
  92.6 1.1 %copy.8 = bf16[192,2,2048]{2,1,0:T(2,128)(2,1)} copy(bf16[192,2,2048]{2,1,0:T(2,128)(2,1)S(1)} %copy-done) | data formatting | bytes 3145728
Async XLA Ops:
  88.8 3.8 %copy-start = (bf16[192,2,2048]{2,1,0:T(2,128)(2,1)S(1)}, bf16[192,2,2048]{2,1,0:T(2,128)(2,1)}, u32[]{:S(2)}) copy-start(bf16[192,2,2048]{2,1,0:T(2,128)(2,1)} %get-tuple-element.5) | copy-start | bytes 4718596

commit v11 on v10

--- a/solution.py
+++ b/solution.py
@@ -97,17 +97,18 @@
     width = x_ref.shape[2] // 2
     depth = 2 * x_ref.shape[1]
 
-    def compute(y, z, x):
+    def compute(y, z, x, sources=(0, 1)):
         w = g_ref[y, z // 2, x, z % 2].reshape(depth, 2 * width)
         koff = pl.multiple_of((y * 2 + z // 2) * depth, depth)
         block = x * 2 + z % 2
-        for src, rows in enumerate((own_ref, partner_ref)):
+        for src in sources:
+            rows = (own_ref, partner_ref)[src]
             first = jnp.dot(rows[:, pl.ds(koff, depth)], w, preferred_element_type=jnp.float32)
             second = jnp.dot(rows[:, pl.ds(band + koff, depth)], w, preferred_element_type=jnp.float32)
             acc[src, 0, block] += first[:, :width] - second[:, width:]
             acc[src, 1, block] += first[:, width:] + second[:, :width]
 
-    def compute_block(held, axis=None, delta=0):
+    def compute_block(held, axis=None, delta=0, sources=(0, 1)):
         at = dict(here)
         if axis is not None:
             at[axis] = lax.rem(at[axis] + delta + RING, RING)
@@ -119,7 +120,7 @@
             for d in full:
                 c[d] = rest % RING
                 rest = rest // RING
-            compute(c["y"], c["z"], c["x"])
+            compute(c["y"], c["z"], c["x"], sources)
             return carry
 
         lax.fori_loop(0, RING ** len(full), body, 0)
@@ -153,6 +154,40 @@
             device_id=partner,
             device_id_type=MESH,
         ).wait_recv()
+
+    def finish(last):
+        lent[...] = acc[1].astype(lent.dtype)
+        give_back = pltpu.make_async_remote_copy(
+            src_ref=lent,
+            dst_ref=back,
+            send_sem=send_sem.at[15],
+            recv_sem=recv_sem.at[15],
+            device_id=partner,
+            device_id_type=MESH,
+        )
+        give_back.start()
+        last()
+        rows = orb_out.shape[0]
+        blocks = acc.shape[2]
+
+        def store(values, h):
+            for a, out in enumerate((orb_out, app_out)):
+                for c in range(blocks):
+                    lane = pl.multiple_of(c * 2 * width + h * width, width)
+                    part = [values[p, c, pl.ds(a * rows, rows), :].astype(out.dtype) for p in range(2)]
+                    out[:, :, pl.ds(lane, width)] = jnp.stack(part, axis=1)
+
+        store(acc.at[0], core)
+        give_back.wait_send()
+        pltpu.make_async_remote_copy(
+            src_ref=lent,
+            dst_ref=back,
+            send_sem=send_sem.at[15],
+            recv_sem=recv_sem.at[15],
+            device_id=partner,
+            device_id_type=MESH,
+        ).wait_recv()
+        store(back, 1 - core)
 
     def run(order):
         held = ()
@@ -198,45 +233,14 @@
             if stage == 0:
                 lend.start()
             if stage == 2:
-                compute_block(held, axis, 2)
+                compute_block(held, axis, 2, (1,))
+                finish(lambda: compute_block(held, axis, 2, (0,)))
             held = held + (axis,)
 
     for index, order in enumerate(ORDERS):
         @pl.when(core == index)
         def _():
             run(order)
-
-    lent[...] = acc[1].astype(lent.dtype)
-    give_back = pltpu.make_async_remote_copy(
-        src_ref=lent,
-        dst_ref=back,
-        send_sem=send_sem.at[15],
-        recv_sem=recv_sem.at[15],
-        device_id=partner,
-        device_id_type=MESH,
-    )
-    give_back.start()
-    rows = orb_out.shape[0]
-    blocks = acc.shape[2]
-
-    def store(values, h):
-        for a, out in enumerate((orb_out, app_out)):
-            for c in range(blocks):
-                lane = pl.multiple_of(c * 2 * width + h * width, width)
-                part = [values[p, c, pl.ds(a * rows, rows), :].astype(out.dtype) for p in range(2)]
-                out[:, :, pl.ds(lane, width)] = jnp.stack(part, axis=1)
-
-    store(acc.at[0], core)
-    give_back.wait_send()
-    pltpu.make_async_remote_copy(
-        src_ref=lent,
-        dst_ref=back,
-        send_sem=send_sem.at[15],
-        recv_sem=recv_sem.at[15],
-        device_id=partner,
-        device_id_type=MESH,
-    ).wait_recv()
-    store(back, 1 - core)
 
 
 def ring_rotate(ritz, orbitals, applied_orbitals):

time: 95.1 us -> 96.9 us (1.019); the launches traced: 93.7 us -> 96.7 us
  Pallas kernels: 88.2 us -> 91.1 us
    pallas_call x1, Pallas kernels: 88.2 us -> 91.1 us  [ring_rotate(): pl.pallas_call(ring_rotate_kernel, out_shape=[out, out], in_specs=[pl.Blo...]
where the time goes in v11:
time: 96.9 us; the launch traced here: 96.7 us
  Pallas kernels  91.1 us (94%)
  local copies, waits for them, and re-layouts  4.89 us (5%)
    pallas_call x1, Pallas kernels, ring_rotate(): pl.pallas_call(ring_rotate_kernel, out_shape=[out, out], in_specs=[pl.Blo...  91.1 us
    unnamed x4, local copies, waits for them, and re-layouts  4.89 us

profile of v11, /device:TPU:0, one launch (start us, length us, event | category | flops | bytes accessed | tf_op | source)
XLA Modules:
  0.0 96.7 jit_solution(6184043510088927445)
XLA Ops:
  0.6 91.1 %shard_map.50 = (bf16[192,2,2048]{2,1,0:T(2,128)(2,1)}, bf16[192,2,2048]{2,1,0:T(2,128)(2,1)}) custom-call(bf16[2,128,256]{2,1,0:T(8,128)(2,1)} %x_ref.1, bf16[192,2,2048]{2,1,0:T(2,128)(2,1)} %orb_ref.1, bf16[192,2,2048]{2,1,0:T(2,128)(2,1)} %app_ref.1), custom_call_target="tpu_custom_call" | custom-call | flops 25769803776 | bytes 12582912 | tf_op jit(solution)/shard_map/pallas_call | solution.py:254
  91.8 0.0 copy-start
  91.8 3.7 %copy.7 = bf16[192,2,2048]{2,1,0:T(2,128)(2,1)} copy(bf16[192,2,2048]{2,1,0:T(2,128)(2,1)} %get-tuple-element.4) | data formatting | bytes 3145728
  95.5 0.0 copy-done
  95.5 1.1 %copy.8 = bf16[192,2,2048]{2,1,0:T(2,128)(2,1)} copy(bf16[192,2,2048]{2,1,0:T(2,128)(2,1)S(1)} %copy-done) | data formatting | bytes 3145728
Async XLA Ops:
  91.8 3.8 %copy-start = (bf16[192,2,2048]{2,1,0:T(2,128)(2,1)S(1)}, bf16[192,2,2048]{2,1,0:T(2,128)(2,1)}, u32[]{:S(2)}) copy-start(bf16[192,2,2048]{2,1,0:T(2,128)(2,1)} %get-tuple-element.5) | copy-start | bytes 4718596

commit v12 on v10

--- a/solution.py
+++ b/solution.py
@@ -19,7 +19,7 @@
 
 
 def ring_rotate_kernel(
-    x_ref, orb_ref, app_ref, orb_out, app_out, g_ref, own_ref, partner_ref, acc, lent, back, send_sem, recv_sem,
+    x_ref, orb_ref, app_ref, own_out, back_out, g_ref, own_ref, partner_ref, acc, lent, back, send_sem, recv_sem,
     local_sem,
 ):
     rc = lax.axis_index("rc")
@@ -216,17 +216,7 @@
         device_id_type=MESH,
     )
     give_back.start()
-    rows = orb_out.shape[0]
-    blocks = acc.shape[2]
-
-    def store(values, h):
-        for a, out in enumerate((orb_out, app_out)):
-            for c in range(blocks):
-                lane = pl.multiple_of(c * 2 * width + h * width, width)
-                part = [values[p, c, pl.ds(a * rows, rows), :].astype(out.dtype) for p in range(2)]
-                out[:, :, pl.ds(lane, width)] = jnp.stack(part, axis=1)
-
-    store(acc.at[0], core)
+    own_out[...] = acc[0].astype(own_out.dtype)
     give_back.wait_send()
     pltpu.make_async_remote_copy(
         src_ref=lent,
@@ -236,7 +226,19 @@
         device_id=partner,
         device_id_type=MESH,
     ).wait_recv()
-    store(back, 1 - core)
+    back_out[...] = back[...]
+
+
+def store_kernel(own_ref, back_ref, orb_out, app_out):
+    core = lax.axis_index("core")
+    rows = orb_out.shape[0]
+    width = own_ref.shape[-1]
+    for h, values in ((core, own_ref), (1 - core, back_ref)):
+        for a, out in enumerate((orb_out, app_out)):
+            for c in range(own_ref.shape[1]):
+                lane = pl.multiple_of(c * 2 * width + h * width, width)
+                part = [values[p, c, pl.ds(a * rows, rows), :] for p in range(2)]
+                out[:, :, pl.ds(lane, width)] = jnp.stack(part, axis=1)
 
 
 def ring_rotate(ritz, orbitals, applied_orbitals):
@@ -244,7 +246,7 @@
     own = orbitals
     units = (RING, 2, RING, 2, 2, ritz.shape[1], ritz.shape[2])
     width = ritz.shape[2] // 2
-    out = jax.ShapeDtypeStruct((rows // 2, 2, band2 // 2), jnp.bfloat16)
+    out = jax.ShapeDtypeStruct((2, 2 * RING, rows, width), jnp.bfloat16)
     vmem = pl.BlockSpec(memory_space=pltpu.VMEM)
     flops = 2 * 2 * rows * band2 * 2 * ritz.shape[2] * 2 * RING
     return pl.pallas_call(
@@ -309,7 +311,15 @@
     rows = orbitals.shape[0]
     band_count = orbitals.shape[2]
 
-    orb_out, app_out = ring_rotate(ritz_matrix, orbitals, applied_orbitals)
+    own_half, back_half = ring_rotate(ritz_matrix, orbitals, applied_orbitals)
+    vmem = pl.BlockSpec(memory_space=pltpu.VMEM)
+    final = jax.ShapeDtypeStruct(orbitals.shape, orbitals.dtype)
+    orb_out, app_out = pl.pallas_call(
+        store_kernel,
+        out_shape=[final, final],
+        in_specs=[vmem, vmem],
+        out_specs=[vmem, vmem],
+    )(own_half, back_half)
     return orb_out, app_out
 
 

time: 95.1 us -> 96.7 us (1.017)
  Pallas kernels: 88.2 us -> 94.6 us
  local copies, waits for them, and re-layouts: 4.89 us -> 0 us
    pallas_call x0 -> x1, Pallas kernels: none -> 9.23 us  [shards(): pl.pallas_call(store_kernel, out_shape=[final, final], in_specs=[vmem, vm...]
    unnamed x4 -> x0, local copies, waits for them, and re-layouts: 4.89 us -> none
    pallas_call x1, Pallas kernels: 88.2 us -> 85.3 us  [ring_rotate(): pl.pallas_call(ring_rotate_kernel, out_shape=[out, out], in_specs=[pl.Blo...]
where the time goes in v12:
time: 96.7 us; the launch traced here: 95.2 us
  Pallas kernels  94.6 us (98%)
    pallas_call x1, Pallas kernels, ring_rotate(): pl.pallas_call(ring_rotate_kernel, out_shape=[out, out], in_specs=[pl.Blo...  85.3 us
    pallas_call x1, Pallas kernels, shards(): pl.pallas_call(store_kernel, out_shape=[final, final], in_specs=[vmem, vm...  9.23 us

profile of v12, /device:TPU:0, one launch (start us, length us, event | category | flops | bytes accessed | tf_op | source)
XLA Modules:
  0.0 95.2 jit_solution(7803124075489124451)
XLA Ops:
  0.6 85.3 %shard_map.50 = (bf16[2,8,384,128]{3,2,1,0:T(8,128)(2,1)}, bf16[2,8,384,128]{3,2,1,0:T(8,128)(2,1)}) custom-call(bf16[2,128,256]{2,1,0:T(8,128)(2,1)} %x_ref.1, bf16[192,2,2048]{2,1,0:T(2,128)(2,1)} %orb_ref.1, bf16[192,2,2048]{2,1,0:T(2,128)(2,1)} %app_ref.1), custom_call_target="tpu_custom_call" | custom-call | flops 25769803776 | bytes 12582912 | tf_op jit(solution)/shard_map/pallas_call | solution.py:252
  86.0 9.2 %shard_map.51 = (bf16[192,2,2048]{2,1,0:T(2,128)(2,1)}, bf16[192,2,2048]{2,1,0:T(2,128)(2,1)}) custom-call(bf16[2,8,384,128]{3,2,1,0:T(8,128)(2,1)} %get-tuple-element.4.own_ref, bf16[2,8,384,128]{3,2,1,0:T(8,128)(2,1)} %get-tuple-element.5.back_ref), custom_call_target="tpu_custom_call" | custom-call | tf_op jit(solution)/shard_map/pallas_call | solution.py:317

commit v13 on v10

--- a/solution.py
+++ b/solution.py
@@ -20,7 +20,7 @@
 
 def ring_rotate_kernel(
     x_ref, orb_ref, app_ref, orb_out, app_out, g_ref, own_ref, partner_ref, acc, lent, back, send_sem, recv_sem,
-    local_sem,
+    local_sem, ring_send, ring_recv,
 ):
     rc = lax.axis_index("rc")
     core = lax.axis_index("core")
@@ -32,10 +32,14 @@
         at[axis] = lax.rem(at[axis] + delta + RING, RING)
         return (at["y"] * 2 + at["z"] // 2, core, at["x"] * 2 + at["z"] % 2)
 
-    def view(held, axis=None, delta=0, half=None):
+    def view(held, axis=None, delta=0, half=None, pin=None):
         at = dict(here)
+        pins = {} if pin is None else {pin[0]: pin[1]}
         if axis is not None:
-            at[axis] = lax.rem(at[axis] + delta + RING, RING)
+            pins[axis] = delta
+        for a, d in pins.items():
+            at[a] = lax.rem(at[a] + d + RING, RING)
+        held = tuple(h for h in held if h not in pins)
         index = []
         split = half is not None
         for dim in DIMS:
@@ -154,21 +158,44 @@
             device_id_type=MESH,
         ).wait_recv()
 
+    def ring(ref, slot, axis, delta):
+        return pltpu.make_async_remote_copy(
+            src_ref=ref,
+            dst_ref=ref,
+            send_sem=ring_send.at[slot],
+            recv_sem=ring_recv.at[slot],
+            device_id=device(axis, delta),
+            device_id_type=MESH,
+        )
+
     def run(order):
         held = ()
+        sent = []
+        pending = []
         for stage, axis in enumerate(order):
-            base = stage * 4
-            src = view(held)
-            out = [
-                remote(src, view(held), base + 0, axis, 1),
-                remote(src, view(held), base + 1, axis, -1),
-            ]
-            for copy in out:
-                copy.start()
+            base = stage * 10
+            if stage == 0:
+                parts = [None]
+            else:
+                prev = order[stage - 1]
+                parts = [(prev, 0), (prev, -1), (prev, 1), (prev, 2)]
+
+            def send_part(i):
+                for j, delta in enumerate((1, -1)):
+                    copy = ring(view(held, pin=parts[i]), base + 4 * j + i, axis, delta)
+                    copy.start()
+                    sent.append(copy)
+
+            for i in range(max(1, len(parts) - 1)):
+                send_part(i)
             if stage == 0:
                 build()
             if stage == 1:
                 acc[...] = jnp.zeros_like(acc)
+            for copy in pending:
+                copy.wait_recv()
+            if stage > 0:
+                send_part(3)
             if stage == 2:
                 lend.wait_send()
                 pltpu.make_async_remote_copy(
@@ -180,26 +207,31 @@
                     device_id_type=MESH,
                 ).wait_recv()
                 compute_block(held)
-            remote(src, view(held, axis, -1), base + 0, axis, -1).wait_recv()
-            remote(src, view(held, axis, 1), base + 1, axis, 1).wait_recv()
+            for i in range(len(parts)):
+                for j, delta in enumerate((1, -1)):
+                    ring(view(held, axis, -delta, pin=parts[i]), base + 4 * j + i, axis, -delta).wait_recv()
             fwd = [
-                remote(view(held, axis, 1, 0), view(held, axis, 1, 0), base + 2, axis, -1),
-                remote(view(held, axis, -1, 1), view(held, axis, -1, 1), base + 3, axis, 1),
+                ring(view(held, axis, 1, 0), base + 8, axis, -1),
+                ring(view(held, axis, -1, 1), base + 9, axis, 1),
             ]
             for copy in fwd:
                 copy.start()
+            sent.extend(fwd)
             if stage == 2:
                 compute_block(held, axis, -1)
                 compute_block(held, axis, 1)
-            remote(view(held, axis, 2, 0), view(held, axis, 2, 0), base + 2, axis, 1).wait_recv()
-            remote(view(held, axis, 2, 1), view(held, axis, 2, 1), base + 3, axis, -1).wait_recv()
-            for copy in out + fwd:
-                copy.wait_send()
+            pending = [
+                ring(view(held, axis, 2, 0), base + 8, axis, 1),
+                ring(view(held, axis, 2, 1), base + 9, axis, -1),
+            ]
             if stage == 0:
                 lend.start()
-            if stage == 2:
-                compute_block(held, axis, 2)
             held = held + (axis,)
+        for copy in pending:
+            copy.wait_recv()
+        for copy in sent:
+            copy.wait_send()
+        compute_block(held[:-1], order[-1], 2)
 
     for index, order in enumerate(ORDERS):
         @pl.when(core == index)
@@ -262,6 +294,8 @@
             pltpu.SemaphoreType.DMA((16,)),
             pltpu.SemaphoreType.DMA((16,)),
             pltpu.SemaphoreType.DMA((2,)),
+            pltpu.SemaphoreType.DMA((30,)),
+            pltpu.SemaphoreType.DMA((30,)),
         ],
         compiler_params=pltpu.CompilerParams(
             collective_id=0, has_side_effects=True, vmem_limit_bytes=60 * 1024 * 1024

time: 95.1 us -> 88.1 us (0.926)
  Pallas kernels: 88.2 us -> 81.2 us
    pallas_call x1, Pallas kernels: 88.2 us -> 81.2 us  [ring_rotate(): pl.pallas_call(ring_rotate_kernel, out_shape=[out, out], in_specs=[pl.Blo...]
where the time goes in v13:
time: 88.1 us; the launch traced here: 86.7 us
  Pallas kernels  81.2 us (92%)
  local copies, waits for them, and re-layouts  4.89 us (6%)
    pallas_call x1, Pallas kernels, ring_rotate(): pl.pallas_call(ring_rotate_kernel, out_shape=[out, out], in_specs=[pl.Blo...  81.2 us
    unnamed x4, local copies, waits for them, and re-layouts  4.89 us

profile of v13, /device:TPU:0, one launch (start us, length us, event | category | flops | bytes accessed | tf_op | source)
XLA Modules:
  0.0 86.7 jit_solution(7802712434776986306)
XLA Ops:
  0.6 81.2 %shard_map.50 = (bf16[192,2,2048]{2,1,0:T(2,128)(2,1)}, bf16[192,2,2048]{2,1,0:T(2,128)(2,1)}) custom-call(bf16[2,128,256]{2,1,0:T(8,128)(2,1)} %x_ref.1, bf16[192,2,2048]{2,1,0:T(2,128)(2,1)} %orb_ref.1, bf16[192,2,2048]{2,1,0:T(2,128)(2,1)} %app_ref.1), custom_call_target="tpu_custom_call" | custom-call | flops 25769803776 | bytes 12582912 | tf_op jit(solution)/shard_map/pallas_call | solution.py:282
  81.8 0.0 copy-start
  81.8 3.7 %copy.7 = bf16[192,2,2048]{2,1,0:T(2,128)(2,1)} copy(bf16[192,2,2048]{2,1,0:T(2,128)(2,1)} %get-tuple-element.4) | data formatting | bytes 3145728
  85.6 0.0 copy-done
  85.6 1.1 %copy.8 = bf16[192,2,2048]{2,1,0:T(2,128)(2,1)} copy(bf16[192,2,2048]{2,1,0:T(2,128)(2,1)S(1)} %copy-done) | data formatting | bytes 3145728
Async XLA Ops:
  81.8 3.8 %copy-start = (bf16[192,2,2048]{2,1,0:T(2,128)(2,1)S(1)}, bf16[192,2,2048]{2,1,0:T(2,128)(2,1)}, u32[]{:S(2)}) copy-start(bf16[192,2,2048]{2,1,0:T(2,128)(2,1)} %get-tuple-element.5) | copy-start | bytes 4718596

commit v14 on v13

--- a/solution.py
+++ b/solution.py
@@ -207,23 +207,22 @@
                     device_id_type=MESH,
                 ).wait_recv()
                 compute_block(held)
+            fwd_base = 30 + stage * 8
             for i in range(len(parts)):
                 for j, delta in enumerate((1, -1)):
                     ring(view(held, axis, -delta, pin=parts[i]), base + 4 * j + i, axis, -delta).wait_recv()
-            fwd = [
-                ring(view(held, axis, 1, 0), base + 8, axis, -1),
-                ring(view(held, axis, -1, 1), base + 9, axis, 1),
-            ]
-            for copy in fwd:
-                copy.start()
-            sent.extend(fwd)
+                    half = 0 if delta == -1 else 1
+                    copy = ring(view(held, axis, -delta, half, parts[i]), fwd_base + 2 * i + j, axis, delta)
+                    copy.start()
+                    sent.append(copy)
             if stage == 2:
                 compute_block(held, axis, -1)
                 compute_block(held, axis, 1)
-            pending = [
-                ring(view(held, axis, 2, 0), base + 8, axis, 1),
-                ring(view(held, axis, 2, 1), base + 9, axis, -1),
-            ]
+            pending = []
+            for i in range(len(parts)):
+                for j, delta in enumerate((1, -1)):
+                    half = 0 if delta == -1 else 1
+                    pending.append(ring(view(held, axis, 2, half, parts[i]), fwd_base + 2 * i + j, axis, -delta))
             if stage == 0:
                 lend.start()
             held = held + (axis,)
@@ -294,8 +293,8 @@
             pltpu.SemaphoreType.DMA((16,)),
             pltpu.SemaphoreType.DMA((16,)),
             pltpu.SemaphoreType.DMA((2,)),
-            pltpu.SemaphoreType.DMA((30,)),
-            pltpu.SemaphoreType.DMA((30,)),
+            pltpu.SemaphoreType.DMA((54,)),
+            pltpu.SemaphoreType.DMA((54,)),
         ],
         compiler_params=pltpu.CompilerParams(
             collective_id=0, has_side_effects=True, vmem_limit_bytes=60 * 1024 * 1024

time: 88.1 us -> 85.4 us (0.969)
  Pallas kernels: 81.2 us -> 78.5 us
    pallas_call x1, Pallas kernels: 81.2 us -> 78.5 us  [ring_rotate(): pl.pallas_call(ring_rotate_kernel, out_shape=[out, out], in_specs=[pl.Blo...]
where the time goes in v14:
time: 85.4 us; the launch traced here: 84.1 us
  Pallas kernels  78.5 us (92%)
  local copies, waits for them, and re-layouts  4.89 us (6%)
    pallas_call x1, Pallas kernels, ring_rotate(): pl.pallas_call(ring_rotate_kernel, out_shape=[out, out], in_specs=[pl.Blo...  78.5 us
    unnamed x4, local copies, waits for them, and re-layouts  4.89 us

profile of v14, /device:TPU:0, one launch (start us, length us, event | category | flops | bytes accessed | tf_op | source)
XLA Modules:
  0.0 84.1 jit_solution(8824419895539105713)
XLA Ops:
  0.6 78.5 %shard_map.50 = (bf16[192,2,2048]{2,1,0:T(2,128)(2,1)}, bf16[192,2,2048]{2,1,0:T(2,128)(2,1)}) custom-call(bf16[2,128,256]{2,1,0:T(8,128)(2,1)} %x_ref.1, bf16[192,2,2048]{2,1,0:T(2,128)(2,1)} %orb_ref.1, bf16[192,2,2048]{2,1,0:T(2,128)(2,1)} %app_ref.1), custom_call_target="tpu_custom_call" | custom-call | flops 25769803776 | bytes 12582912 | tf_op jit(solution)/shard_map/pallas_call | solution.py:281
  79.1 0.0 copy-start
  79.2 3.7 %copy.7 = bf16[192,2,2048]{2,1,0:T(2,128)(2,1)} copy(bf16[192,2,2048]{2,1,0:T(2,128)(2,1)} %get-tuple-element.4) | data formatting | bytes 3145728
  82.9 0.0 copy-done
  82.9 1.1 %copy.8 = bf16[192,2,2048]{2,1,0:T(2,128)(2,1)} copy(bf16[192,2,2048]{2,1,0:T(2,128)(2,1)S(1)} %copy-done) | data formatting | bytes 3145728
Async XLA Ops:
  79.1 3.8 %copy-start = (bf16[192,2,2048]{2,1,0:T(2,128)(2,1)S(1)}, bf16[192,2,2048]{2,1,0:T(2,128)(2,1)}, u32[]{:S(2)}) copy-start(bf16[192,2,2048]{2,1,0:T(2,128)(2,1)} %get-tuple-element.5) | copy-start | bytes 4718596

commit v15 on v14

--- a/solution.py
+++ b/solution.py
@@ -111,11 +111,14 @@
             acc[src, 0, block] += first[:, :width] - second[:, width:]
             acc[src, 1, block] += first[:, width:] + second[:, :width]
 
-    def compute_block(held, axis=None, delta=0):
+    def compute_block(held, axis=None, delta=0, pin=None):
         at = dict(here)
+        pins = {} if pin is None else {pin[0]: pin[1]}
         if axis is not None:
-            at[axis] = lax.rem(at[axis] + delta + RING, RING)
-        full = [d for d in ("y", "z", "x") if d in held]
+            pins[axis] = delta
+        for a, d in pins.items():
+            at[a] = lax.rem(at[a] + d + RING, RING)
+        full = [d for d in ("y", "z", "x") if d in held and d not in pins]
 
         def body(i, carry):
             c = dict(at)
@@ -226,11 +229,12 @@
             if stage == 0:
                 lend.start()
             held = held + (axis,)
-        for copy in pending:
-            copy.wait_recv()
+        for i in range(len(parts)):
+            pending[2 * i].wait_recv()
+            pending[2 * i + 1].wait_recv()
+            compute_block(held[:-1], order[-1], 2, parts[i])
         for copy in sent:
             copy.wait_send()
-        compute_block(held[:-1], order[-1], 2)
 
     for index, order in enumerate(ORDERS):
         @pl.when(core == index)

time: 85.4 us -> 85.4 us (level)
  no operation moved by 1% of the time
where the time goes in v15:
time: 85.4 us; the launch traced here: 84 us
  Pallas kernels  78.5 us (92%)
  local copies, waits for them, and re-layouts  4.89 us (6%)
    pallas_call x1, Pallas kernels, ring_rotate(): pl.pallas_call(ring_rotate_kernel, out_shape=[out, out], in_specs=[pl.Blo...  78.5 us
    unnamed x4, local copies, waits for them, and re-layouts  4.89 us

profile of v15, /device:TPU:0, one launch (start us, length us, event | category | flops | bytes accessed | tf_op | source)
XLA Modules:
  0.0 84.0 jit_solution(16838044412772519515)
XLA Ops:
  0.6 78.5 %shard_map.50 = (bf16[192,2,2048]{2,1,0:T(2,128)(2,1)}, bf16[192,2,2048]{2,1,0:T(2,128)(2,1)}) custom-call(bf16[2,128,256]{2,1,0:T(8,128)(2,1)} %x_ref.1, bf16[192,2,2048]{2,1,0:T(2,128)(2,1)} %orb_ref.1, bf16[192,2,2048]{2,1,0:T(2,128)(2,1)} %app_ref.1), custom_call_target="tpu_custom_call" | custom-call | flops 25769803776 | bytes 12582912 | tf_op jit(solution)/shard_map/pallas_call | solution.py:285
  79.1 0.0 copy-start
  79.1 3.7 %copy.7 = bf16[192,2,2048]{2,1,0:T(2,128)(2,1)} copy(bf16[192,2,2048]{2,1,0:T(2,128)(2,1)} %get-tuple-element.4) | data formatting | bytes 3145728
  82.9 0.0 copy-done
  82.9 1.1 %copy.8 = bf16[192,2,2048]{2,1,0:T(2,128)(2,1)} copy(bf16[192,2,2048]{2,1,0:T(2,128)(2,1)S(1)} %copy-done) | data formatting | bytes 3145728
Async XLA Ops:
  79.1 3.8 %copy-start = (bf16[192,2,2048]{2,1,0:T(2,128)(2,1)S(1)}, bf16[192,2,2048]{2,1,0:T(2,128)(2,1)}, u32[]{:S(2)}) copy-start(bf16[192,2,2048]{2,1,0:T(2,128)(2,1)} %get-tuple-element.5) | copy-start | bytes 4718596

commit v16 on v14

--- a/solution.py
+++ b/solution.py
@@ -146,17 +146,36 @@
         )
         swap.start()
         moves.append((local, swap, unit.at[1 - core, :, pl.ds(p * width, width)], p))
-    for local, swap, dst, p in moves:
-        local.wait()
-        swap.wait_send()
-        pltpu.make_async_remote_copy(
-            src_ref=x_ref.at[p, :, pl.ds(give, width)],
+
+    def settle():
+        for local, swap, dst, p in moves:
+            local.wait()
+            swap.wait_send()
+            pltpu.make_async_remote_copy(
+                src_ref=x_ref.at[p, :, pl.ds(give, width)],
+                dst_ref=dst,
+                send_sem=send_sem.at[12 + p],
+                recv_sem=recv_sem.at[12 + p],
+                device_id=partner,
+                device_id_type=MESH,
+            ).wait_recv()
+
+    def ring2(src, dst, slot, axis, delta):
+        return pltpu.make_async_remote_copy(
+            src_ref=src,
             dst_ref=dst,
-            send_sem=send_sem.at[12 + p],
-            recv_sem=recv_sem.at[12 + p],
-            device_id=partner,
+            send_sem=ring_send.at[slot],
+            recv_sem=ring_recv.at[slot],
+            device_id=device(axis, delta),
             device_id_type=MESH,
-        ).wait_recv()
+        )
+
+    def first_pieces(axis, delta, side):
+        at = view((), axis, side) if side else unit
+        return [
+            (x_ref.at[p, :, pl.ds(keep, width)], at.at[core, :, pl.ds(p * width, width)], 4 * (0 if delta == 1 else 1) + p)
+            for p in range(2)
+        ] + [(at.at[1 - core], at.at[1 - core], 4 * (0 if delta == 1 else 1) + 2)]
 
     def ring(ref, slot, axis, delta):
         return pltpu.make_async_remote_copy(
@@ -186,10 +205,24 @@
                     copy.start()
                     sent.append(copy)
 
-            for i in range(max(1, len(parts) - 1)):
+            if stage == 0:
+                for delta in (1, -1):
+                    for src, dst, slot in first_pieces(axis, delta, 0)[:2]:
+                        copy = ring2(src, dst, slot, axis, delta)
+                        copy.start()
+                        sent.append(copy)
+                settle()
+                for delta in (1, -1):
+                    for src, dst, slot in first_pieces(axis, delta, 0)[2:]:
+                        copy = ring2(src, dst, slot, axis, delta)
+                        copy.start()
+                        sent.append(copy)
+                build()
+                for delta in (1, -1):
+                    for src, dst, slot in first_pieces(axis, delta, -delta):
+                        ring2(src, dst, slot, axis, -delta).wait_recv()
+            for i in range(len(parts) - 1):
                 send_part(i)
-            if stage == 0:
-                build()
             if stage == 1:
                 acc[...] = jnp.zeros_like(acc)
             for copy in pending:
@@ -210,7 +243,8 @@
             fwd_base = 30 + stage * 8
             for i in range(len(parts)):
                 for j, delta in enumerate((1, -1)):
-                    ring(view(held, axis, -delta, pin=parts[i]), base + 4 * j + i, axis, -delta).wait_recv()
+                    if stage > 0:
+                        ring(view(held, axis, -delta, pin=parts[i]), base + 4 * j + i, axis, -delta).wait_recv()
                     half = 0 if delta == -1 else 1
                     copy = ring(view(held, axis, -delta, half, parts[i]), fwd_base + 2 * i + j, axis, delta)
                     copy.start()

time: 85.4 us -> 85.4 us (level)
  no operation moved by 1% of the time
where the time goes in v16:
time: 85.4 us; the launch traced here: 84.1 us
  Pallas kernels  78.5 us (92%)
  local copies, waits for them, and re-layouts  4.89 us (6%)
    pallas_call x1, Pallas kernels, ring_rotate(): pl.pallas_call(ring_rotate_kernel, out_shape=[out, out], in_specs=[pl.Blo...  78.5 us
    unnamed x4, local copies, waits for them, and re-layouts  4.89 us

profile of v16, /device:TPU:0, one launch (start us, length us, event | category | flops | bytes accessed | tf_op | source)
XLA Modules:
  0.0 84.1 jit_solution(14702275842310331929)
XLA Ops:
  0.6 78.5 %shard_map.50 = (bf16[192,2,2048]{2,1,0:T(2,128)(2,1)}, bf16[192,2,2048]{2,1,0:T(2,128)(2,1)}) custom-call(bf16[2,128,256]{2,1,0:T(8,128)(2,1)} %x_ref.1, bf16[192,2,2048]{2,1,0:T(2,128)(2,1)} %orb_ref.1, bf16[192,2,2048]{2,1,0:T(2,128)(2,1)} %app_ref.1), custom_call_target="tpu_custom_call" | custom-call | flops 25769803776 | bytes 12582912 | tf_op jit(solution)/shard_map/pallas_call | solution.py:315
  79.2 0.0 copy-start
  79.2 3.7 %copy.7 = bf16[192,2,2048]{2,1,0:T(2,128)(2,1)} copy(bf16[192,2,2048]{2,1,0:T(2,128)(2,1)} %get-tuple-element.4) | data formatting | bytes 3145728
  82.9 0.0 copy-done
  82.9 1.1 %copy.8 = bf16[192,2,2048]{2,1,0:T(2,128)(2,1)} copy(bf16[192,2,2048]{2,1,0:T(2,128)(2,1)S(1)} %copy-done) | data formatting | bytes 3145728
Async XLA Ops:
  79.2 3.8 %copy-start = (bf16[192,2,2048]{2,1,0:T(2,128)(2,1)S(1)}, bf16[192,2,2048]{2,1,0:T(2,128)(2,1)}, u32[]{:S(2)}) copy-start(bf16[192,2,2048]{2,1,0:T(2,128)(2,1)} %get-tuple-element.5) | copy-start | bytes 4718596

commit v17 on v15

--- a/solution.py
+++ b/solution.py
@@ -209,7 +209,6 @@
                     device_id=partner,
                     device_id_type=MESH,
                 ).wait_recv()
-                compute_block(held)
             fwd_base = 30 + stage * 8
             for i in range(len(parts)):
                 for j, delta in enumerate((1, -1)):
@@ -218,6 +217,8 @@
                     copy = ring(view(held, axis, -delta, half, parts[i]), fwd_base + 2 * i + j, axis, delta)
                     copy.start()
                     sent.append(copy)
+                if stage == 2:
+                    compute_block(held, pin=parts[i])
             if stage == 2:
                 compute_block(held, axis, -1)
                 compute_block(held, axis, 1)
@@ -229,12 +230,11 @@
             if stage == 0:
                 lend.start()
             held = held + (axis,)
-        for i in range(len(parts)):
-            pending[2 * i].wait_recv()
-            pending[2 * i + 1].wait_recv()
-            compute_block(held[:-1], order[-1], 2, parts[i])
+        for copy in pending:
+            copy.wait_recv()
         for copy in sent:
             copy.wait_send()
+        compute_block(held[:-1], order[-1], 2)
 
     for index, order in enumerate(ORDERS):
         @pl.when(core == index)

time: 85.4 us -> 86.9 us (1.018)
  Pallas kernels: 78.5 us -> 80 us
    pallas_call x1, Pallas kernels: 78.5 us -> 80 us  [ring_rotate(): pl.pallas_call(ring_rotate_kernel, out_shape=[out, out], in_specs=[pl.Blo...]
where the time goes in v17:
time: 86.9 us; the launch traced here: 85.6 us
  Pallas kernels  80 us (92%)
  local copies, waits for them, and re-layouts  4.89 us (6%)
    pallas_call x1, Pallas kernels, ring_rotate(): pl.pallas_call(ring_rotate_kernel, out_shape=[out, out], in_specs=[pl.Blo...  80 us
    unnamed x4, local copies, waits for them, and re-layouts  4.89 us

profile of v17, /device:TPU:0, one launch (start us, length us, event | category | flops | bytes accessed | tf_op | source)
XLA Modules:
  0.0 85.6 jit_solution(13455175802497941318)
XLA Ops:
  0.6 80.0 %shard_map.50 = (bf16[192,2,2048]{2,1,0:T(2,128)(2,1)}, bf16[192,2,2048]{2,1,0:T(2,128)(2,1)}) custom-call(bf16[2,128,256]{2,1,0:T(8,128)(2,1)} %x_ref.1, bf16[192,2,2048]{2,1,0:T(2,128)(2,1)} %orb_ref.1, bf16[192,2,2048]{2,1,0:T(2,128)(2,1)} %app_ref.1), custom_call_target="tpu_custom_call" | custom-call | flops 25769803776 | bytes 12582912 | tf_op jit(solution)/shard_map/pallas_call | solution.py:285
  80.7 0.0 copy-start
  80.7 3.7 %copy.7 = bf16[192,2,2048]{2,1,0:T(2,128)(2,1)} copy(bf16[192,2,2048]{2,1,0:T(2,128)(2,1)} %get-tuple-element.4) | data formatting | bytes 3145728
  84.4 0.0 copy-done
  84.4 1.1 %copy.8 = bf16[192,2,2048]{2,1,0:T(2,128)(2,1)} copy(bf16[192,2,2048]{2,1,0:T(2,128)(2,1)S(1)} %copy-done) | data formatting | bytes 3145728
Async XLA Ops:
  80.7 3.8 %copy-start = (bf16[192,2,2048]{2,1,0:T(2,128)(2,1)S(1)}, bf16[192,2,2048]{2,1,0:T(2,128)(2,1)}, u32[]{:S(2)}) copy-start(bf16[192,2,2048]{2,1,0:T(2,128)(2,1)} %get-tuple-element.5) | copy-start | bytes 4718596

commit v18 on v14

--- a/solution.py
+++ b/solution.py
@@ -188,9 +188,9 @@
 
             for i in range(max(1, len(parts) - 1)):
                 send_part(i)
-            if stage == 0:
+            if stage == 1:
                 build()
-            if stage == 1:
+                lend.start()
                 acc[...] = jnp.zeros_like(acc)
             for copy in pending:
                 copy.wait_recv()
@@ -223,8 +223,6 @@
                 for j, delta in enumerate((1, -1)):
                     half = 0 if delta == -1 else 1
                     pending.append(ring(view(held, axis, 2, half, parts[i]), fwd_base + 2 * i + j, axis, -delta))
-            if stage == 0:
-                lend.start()
             held = held + (axis,)
         for copy in pending:
             copy.wait_recv()

time: 85.4 us -> 85 us (level)
  no operation moved by 1% of the time
where the time goes in v18:
time: 85 us; the launch traced here: 83.7 us
  Pallas kernels  78.1 us (92%)
  local copies, waits for them, and re-layouts  4.89 us (6%)
    pallas_call x1, Pallas kernels, ring_rotate(): pl.pallas_call(ring_rotate_kernel, out_shape=[out, out], in_specs=[pl.Blo...  78.1 us
    unnamed x4, local copies, waits for them, and re-layouts  4.89 us

profile of v18, /device:TPU:0, one launch (start us, length us, event | category | flops | bytes accessed | tf_op | source)
XLA Modules:
  0.0 83.7 jit_solution(5377528101374381336)
XLA Ops:
  0.6 78.1 %shard_map.50 = (bf16[192,2,2048]{2,1,0:T(2,128)(2,1)}, bf16[192,2,2048]{2,1,0:T(2,128)(2,1)}) custom-call(bf16[2,128,256]{2,1,0:T(8,128)(2,1)} %x_ref.1, bf16[192,2,2048]{2,1,0:T(2,128)(2,1)} %orb_ref.1, bf16[192,2,2048]{2,1,0:T(2,128)(2,1)} %app_ref.1), custom_call_target="tpu_custom_call" | custom-call | flops 25769803776 | bytes 12582912 | tf_op jit(solution)/shard_map/pallas_call | solution.py:279
  78.8 0.0 copy-start
  78.8 3.7 %copy.7 = bf16[192,2,2048]{2,1,0:T(2,128)(2,1)} copy(bf16[192,2,2048]{2,1,0:T(2,128)(2,1)} %get-tuple-element.4) | data formatting | bytes 3145728
  82.5 0.0 copy-done
  82.5 1.1 %copy.8 = bf16[192,2,2048]{2,1,0:T(2,128)(2,1)} copy(bf16[192,2,2048]{2,1,0:T(2,128)(2,1)S(1)} %copy-done) | data formatting | bytes 3145728
Async XLA Ops:
  78.8 3.8 %copy-start = (bf16[192,2,2048]{2,1,0:T(2,128)(2,1)S(1)}, bf16[192,2,2048]{2,1,0:T(2,128)(2,1)}, u32[]{:S(2)}) copy-start(bf16[192,2,2048]{2,1,0:T(2,128)(2,1)} %get-tuple-element.5) | copy-start | bytes 4718596

commit v19 on v18

--- a/solution.py
+++ b/solution.py
@@ -157,6 +157,22 @@
             device_id=partner,
             device_id_type=MESH,
         ).wait_recv()
+
+    rows = orb_out.shape[0]
+    blocks = acc.shape[2]
+
+    def store_block(values, h, c):
+        for a, out in enumerate((orb_out, app_out)):
+            lane = pl.multiple_of(c * 2 * width + h * width, width)
+            part = [values[p, c, pl.ds(a * rows, rows), :].astype(out.dtype) for p in range(2)]
+            out[:, :, pl.ds(lane, width)] = jnp.stack(part, axis=1)
+
+    def early(c, last):
+        if last == "z":
+            return c % 2 != here["z"] % 2
+        if last == "x":
+            return c // 2 != lax.rem(here["x"] + 2, RING)
+        return core < 0
 
     def ring(ref, slot, axis, delta):
         return pltpu.make_async_remote_copy(
@@ -224,6 +240,11 @@
                     half = 0 if delta == -1 else 1
                     pending.append(ring(view(held, axis, 2, half, parts[i]), fwd_base + 2 * i + j, axis, -delta))
             held = held + (axis,)
+        for c in range(blocks):
+            @pl.when(early(c, order[-1]))
+            def _():
+                store_block(acc.at[0], core, c)
+
         for copy in pending:
             copy.wait_recv()
         for copy in sent:
@@ -245,17 +266,15 @@
         device_id_type=MESH,
     )
     give_back.start()
-    rows = orb_out.shape[0]
-    blocks = acc.shape[2]
-
-    def store(values, h):
-        for a, out in enumerate((orb_out, app_out)):
-            for c in range(blocks):
-                lane = pl.multiple_of(c * 2 * width + h * width, width)
-                part = [values[p, c, pl.ds(a * rows, rows), :].astype(out.dtype) for p in range(2)]
-                out[:, :, pl.ds(lane, width)] = jnp.stack(part, axis=1)
-
-    store(acc.at[0], core)
+    for c in range(blocks):
+        late = early(c, ORDERS[0][-1])
+        for index, order in enumerate(ORDERS[1:], 1):
+            late = jnp.where(core == index, early(c, order[-1]), late)
+
+        @pl.when(jnp.logical_not(late))
+        def _():
+            store_block(acc.at[0], core, c)
+
     give_back.wait_send()
     pltpu.make_async_remote_copy(
         src_ref=lent,
@@ -265,7 +284,8 @@
         device_id=partner,
         device_id_type=MESH,
     ).wait_recv()
-    store(back, 1 - core)
+    for c in range(blocks):
+        store_block(back, 1 - core, c)
 
 
 def ring_rotate(ritz, orbitals, applied_orbitals):

time: 85 us -> 86.6 us (1.019)
  Pallas kernels: 78.1 us -> 79.6 us
    pallas_call x1, Pallas kernels: 78.1 us -> 79.6 us  [ring_rotate(): pl.pallas_call(ring_rotate_kernel, out_shape=[out, out], in_specs=[pl.Blo...]
where the time goes in v19:
time: 86.6 us; the launch traced here: 85.1 us
  Pallas kernels  79.6 us (92%)
  local copies, waits for them, and re-layouts  4.89 us (6%)
    pallas_call x1, Pallas kernels, ring_rotate(): pl.pallas_call(ring_rotate_kernel, out_shape=[out, out], in_specs=[pl.Blo...  79.6 us
    unnamed x4, local copies, waits for them, and re-layouts  4.89 us

profile of v19, /device:TPU:0, one launch (start us, length us, event | category | flops | bytes accessed | tf_op | source)
XLA Modules:
  0.0 85.1 jit_solution(3648512006707893086)
XLA Ops:
  0.6 79.6 %shard_map.50 = (bf16[192,2,2048]{2,1,0:T(2,128)(2,1)}, bf16[192,2,2048]{2,1,0:T(2,128)(2,1)}) custom-call(bf16[2,128,256]{2,1,0:T(8,128)(2,1)} %x_ref.1, bf16[192,2,2048]{2,1,0:T(2,128)(2,1)} %orb_ref.1, bf16[192,2,2048]{2,1,0:T(2,128)(2,1)} %app_ref.1), custom_call_target="tpu_custom_call" | custom-call | flops 25769803776 | bytes 12582912 | tf_op jit(solution)/shard_map/pallas_call | solution.py:299
  80.2 0.0 copy-start
  80.2 3.7 %copy.7 = bf16[192,2,2048]{2,1,0:T(2,128)(2,1)} copy(bf16[192,2,2048]{2,1,0:T(2,128)(2,1)} %get-tuple-element.4) | data formatting | bytes 3145728
  84.0 0.0 copy-done
  84.0 1.1 %copy.8 = bf16[192,2,2048]{2,1,0:T(2,128)(2,1)} copy(bf16[192,2,2048]{2,1,0:T(2,128)(2,1)S(1)} %copy-done) | data formatting | bytes 3145728
Async XLA Ops:
  80.2 3.8 %copy-start = (bf16[192,2,2048]{2,1,0:T(2,128)(2,1)S(1)}, bf16[192,2,2048]{2,1,0:T(2,128)(2,1)}, u32[]{:S(2)}) copy-start(bf16[192,2,2048]{2,1,0:T(2,128)(2,1)} %get-tuple-element.5) | copy-start | bytes 4718596

commit v20 on v18

--- a/solution.py
+++ b/solution.py
@@ -188,10 +188,11 @@
 
             for i in range(max(1, len(parts) - 1)):
                 send_part(i)
+            if stage == 0:
+                acc[...] = jnp.zeros_like(acc)
             if stage == 1:
                 build()
                 lend.start()
-                acc[...] = jnp.zeros_like(acc)
             for copy in pending:
                 copy.wait_recv()
             if stage > 0:

time: 85 us -> 84.6 us (level)
  no operation moved by 1% of the time
where the time goes in v20:
time: 84.6 us; the launch traced here: 83.3 us
  Pallas kernels  77.7 us (92%)
  local copies, waits for them, and re-layouts  4.89 us (6%)
    pallas_call x1, Pallas kernels, ring_rotate(): pl.pallas_call(ring_rotate_kernel, out_shape=[out, out], in_specs=[pl.Blo...  77.7 us
    unnamed x4, local copies, waits for them, and re-layouts  4.89 us

profile of v20, /device:TPU:0, one launch (start us, length us, event | category | flops | bytes accessed | tf_op | source)
XLA Modules:
  0.0 83.3 jit_solution(10803933666310276970)
XLA Ops:
  0.6 77.7 %shard_map.50 = (bf16[192,2,2048]{2,1,0:T(2,128)(2,1)}, bf16[192,2,2048]{2,1,0:T(2,128)(2,1)}) custom-call(bf16[2,128,256]{2,1,0:T(8,128)(2,1)} %x_ref.1, bf16[192,2,2048]{2,1,0:T(2,128)(2,1)} %orb_ref.1, bf16[192,2,2048]{2,1,0:T(2,128)(2,1)} %app_ref.1), custom_call_target="tpu_custom_call" | custom-call | flops 25769803776 | bytes 12582912 | tf_op jit(solution)/shard_map/pallas_call | solution.py:280
  78.4 0.0 copy-start
  78.4 3.7 %copy.7 = bf16[192,2,2048]{2,1,0:T(2,128)(2,1)} copy(bf16[192,2,2048]{2,1,0:T(2,128)(2,1)} %get-tuple-element.4) | data formatting | bytes 3145728
  82.1 0.0 copy-done
  82.1 1.1 %copy.8 = bf16[192,2,2048]{2,1,0:T(2,128)(2,1)} copy(bf16[192,2,2048]{2,1,0:T(2,128)(2,1)S(1)} %copy-done) | data formatting | bytes 3145728
Async XLA Ops:
  78.4 3.8 %copy-start = (bf16[192,2,2048]{2,1,0:T(2,128)(2,1)S(1)}, bf16[192,2,2048]{2,1,0:T(2,128)(2,1)}, u32[]{:S(2)}) copy-start(bf16[192,2,2048]{2,1,0:T(2,128)(2,1)} %get-tuple-element.5) | copy-start | bytes 4718596

commit v21 on v20

--- a/solution.py
+++ b/solution.py
@@ -79,9 +79,10 @@
     pl.semaphore_signal(barrier, 1, device_id=partner, device_id_type=MESH)
     pl.semaphore_wait(barrier, 7)
 
+    half_rows = own_ref.shape[0] // 2
     lend = pltpu.make_async_remote_copy(
-        src_ref=own_ref,
-        dst_ref=partner_ref,
+        src_ref=own_ref.at[pl.ds(0, half_rows)],
+        dst_ref=own_ref.at[pl.ds(half_rows, half_rows)],
         send_sem=send_sem.at[14],
         recv_sem=recv_sem.at[14],
         device_id=partner,
@@ -105,11 +106,10 @@
         w = g_ref[y, z // 2, x, z % 2].reshape(depth, 2 * width)
         koff = pl.multiple_of((y * 2 + z // 2) * depth, depth)
         block = x * 2 + z % 2
-        for src, rows in enumerate((own_ref, partner_ref)):
-            first = jnp.dot(rows[:, pl.ds(koff, depth)], w, preferred_element_type=jnp.float32)
-            second = jnp.dot(rows[:, pl.ds(band + koff, depth)], w, preferred_element_type=jnp.float32)
-            acc[src, 0, block] += first[:, :width] - second[:, width:]
-            acc[src, 1, block] += first[:, width:] + second[:, :width]
+        first = jnp.dot(own_ref[:, pl.ds(koff, depth)], w, preferred_element_type=jnp.float32)
+        second = jnp.dot(own_ref[:, pl.ds(band + koff, depth)], w, preferred_element_type=jnp.float32)
+        acc[0, block] += first[:, :width] - second[:, width:]
+        acc[1, block] += first[:, width:] + second[:, :width]
 
     def compute_block(held, axis=None, delta=0):
         at = dict(here)
@@ -200,8 +200,8 @@
             if stage == 2:
                 lend.wait_send()
                 pltpu.make_async_remote_copy(
-                    src_ref=own_ref,
-                    dst_ref=partner_ref,
+                    src_ref=own_ref.at[pl.ds(0, half_rows)],
+                    dst_ref=own_ref.at[pl.ds(half_rows, half_rows)],
                     send_sem=send_sem.at[14],
                     recv_sem=recv_sem.at[14],
                     device_id=partner,
@@ -236,7 +236,7 @@
         def _():
             run(order)
 
-    lent[...] = acc[1].astype(lent.dtype)
+    lent[...] = acc[:, :, pl.ds(half_rows, half_rows), :].astype(lent.dtype)
     give_back = pltpu.make_async_remote_copy(
         src_ref=lent,
         dst_ref=back,
@@ -247,7 +247,7 @@
     )
     give_back.start()
     rows = orb_out.shape[0]
-    blocks = acc.shape[2]
+    blocks = acc.shape[1]
 
     def store(values, h):
         for a, out in enumerate((orb_out, app_out)):
@@ -256,7 +256,7 @@
                 part = [values[p, c, pl.ds(a * rows, rows), :].astype(out.dtype) for p in range(2)]
                 out[:, :, pl.ds(lane, width)] = jnp.stack(part, axis=1)
 
-    store(acc.at[0], core)
+    store(acc, core)
     give_back.wait_send()
     pltpu.make_async_remote_copy(
         src_ref=lent,
@@ -284,9 +284,9 @@
         out_specs=[vmem, vmem],
         scratch_shapes=[
             pltpu.VMEM(units, ritz.dtype),
+            pltpu.VMEM((2 * rows, band2), own.dtype),
             pltpu.VMEM((rows, band2), own.dtype),
-            pltpu.VMEM((rows, band2), own.dtype),
-            pltpu.VMEM((2, 2, 2 * RING, rows, width), jnp.float32),
+            pltpu.VMEM((2, 2 * RING, 2 * rows, width), jnp.float32),
             pltpu.VMEM((2, 2 * RING, rows, width), jnp.bfloat16),
             pltpu.VMEM((2, 2 * RING, rows, width), jnp.bfloat16),
             pltpu.SemaphoreType.DMA((16,)),

time: 84.6 us -> 84.4 us (level)
  no operation moved by 1% of the time
where the time goes in v21:
time: 84.4 us; the launch traced here: 83 us
  Pallas kernels  77.5 us (92%)
  local copies, waits for them, and re-layouts  4.89 us (6%)
    pallas_call x1, Pallas kernels, ring_rotate(): pl.pallas_call(ring_rotate_kernel, out_shape=[out, out], in_specs=[pl.Blo...  77.5 us
    unnamed x4, local copies, waits for them, and re-layouts  4.89 us

profile of v21, /device:TPU:0, one launch (start us, length us, event | category | flops | bytes accessed | tf_op | source)
XLA Modules:
  0.0 83.0 jit_solution(13973035231055460918)
XLA Ops:
  0.6 77.5 %shard_map.50 = (bf16[192,2,2048]{2,1,0:T(2,128)(2,1)}, bf16[192,2,2048]{2,1,0:T(2,128)(2,1)}) custom-call(bf16[2,128,256]{2,1,0:T(8,128)(2,1)} %x_ref.1, bf16[192,2,2048]{2,1,0:T(2,128)(2,1)} %orb_ref.1, bf16[192,2,2048]{2,1,0:T(2,128)(2,1)} %app_ref.1), custom_call_target="tpu_custom_call" | custom-call | flops 25769803776 | bytes 12582912 | tf_op jit(solution)/shard_map/pallas_call | solution.py:280
  78.1 0.0 copy-start
  78.1 3.7 %copy.7 = bf16[192,2,2048]{2,1,0:T(2,128)(2,1)} copy(bf16[192,2,2048]{2,1,0:T(2,128)(2,1)} %get-tuple-element.4) | data formatting | bytes 3145728
  81.9 0.0 copy-done
  81.9 1.1 %copy.8 = bf16[192,2,2048]{2,1,0:T(2,128)(2,1)} copy(bf16[192,2,2048]{2,1,0:T(2,128)(2,1)S(1)} %copy-done) | data formatting | bytes 3145728
Async XLA Ops:
  78.1 3.8 %copy-start = (bf16[192,2,2048]{2,1,0:T(2,128)(2,1)S(1)}, bf16[192,2,2048]{2,1,0:T(2,128)(2,1)}, u32[]{:S(2)}) copy-start(bf16[192,2,2048]{2,1,0:T(2,128)(2,1)} %get-tuple-element.5) | copy-start | bytes 4718596
